TPU v7x, 32 devices: a whole 2x2x4 slice. The times are simulated.
32 devices in a mesh: ctx: 16 (over z, x, core), tp: 2 (over y).
Axes of the slice: x: 2, y: 2, z: 4, core: 2. Of those that a mesh axis runs over, the one named last changes fastest.
Arguments:
- inner_input: bfloat16 [2048, 8192], P('ctx', 'tp'), may hold values from -6 to 6
- gate_input: bfloat16 [2048, 8192], P('ctx', 'tp'), may hold values from -6 to 6
- state_inputs: bfloat16 [2, 2048, 1024], P(None, 'ctx', 'tp'), may hold values from -6 to 6
- step_size: float32 [128, 2048], P('tp', 'ctx'), may hold values from 0.5 to 2
- resets: int32 [2048], P('ctx'), may hold values 0 or 1
- decay_rate: float32 [128], P('tp'), may hold values from 0 to 0.04
- skip_gain: float32 [128], P('tp'), may hold values from 0.5 to 1.5
- conv_inner: float32 [4, 8192], P(None, 'tp'), may hold values from -3 to 3
- conv_state: float32 [2, 4, 1024], P(None, None, 'tp'), may hold values from -3 to 3
- norm_gain: float32 [8192], P('tp'), may hold values from 0.5 to 1.5
- out_weight: bfloat16 [8192, 4096], P('tp', 'ctx'), may hold values from -0.0625 to 0.0625
- residual: bfloat16 [2048, 4096], P('ctx', 'tp'), may hold values from -6 to 6
- final_gain: float32 [4096], replicated, may hold values from 0.5 to 1.5
- head_weight: bfloat16 [4096, 65536], P(None, ('ctx', 'tp')), may hold values from -8 to 8
- scored: int32 [128], P('ctx'), may hold values from 0 to 2047, as said below
- targets: int32 [128], replicated, may hold values from 0 to 65535
- policy_logprob: float32 [128], replicated, may hold values from -20 to -10
Outputs:
- ref_logprob: float32 [128], replicated
- token_kl: float32 [128], replicated
Inputs may be any that keep to these rules, and one draw needn't show every extreme that they name: `scored`: entries j * 8 to (j + 1) * 8 - 1 are distinct positions in j * 128 to (j + 1) * 128 - 1.
All inputs are finite; a program needn't handle non-finite values. No bound on the sum of `resets` on one device may be relied on, other than what follows from the above.
Results may differ from a plain program's by a relative error of at most 0.00215.
The roundings to bfloat16 on the way count: a program that leaves them out, or rounds other values in their place, can miss the bound.
Values may be sent and summed in bfloat16 or wider, within the bound.
A program may use at most 128 MiB of HBM per device.

v0:
```python
import jax
import jax.numpy as jnp
from jax import lax
from jax.sharding import PartitionSpec as P

HEAD_DIM = 64
STATE = 128
SPAN = 128


epsilon = 1e-05
precise = lax.Precision.HIGHEST


def passed_along(shard, axis, by):
    count = lax.axis_size(axis)
    pairs = [(i, i + by) for i in range(count) if 0 <= i + by < count]
    return lax.ppermute(shard, axis, pairs)


def carried_in(part, axis, combine, identity):
    place = lax.axis_index(axis)
    gathered = jax.tree.map(lambda a: lax.all_gather(a, axis), part)
    state = jax.tree.map(lambda a, e: jnp.zeros_like(a) + jnp.asarray(e, a.dtype), part, identity)

    def one(hop, state):
        return combine(
            state, jax.tree.map(lambda a: lax.dynamic_index_in_dim(a, hop, 0, False), gathered)
        )

    return lax.fori_loop(0, place, one, state)


def causal_filter(stream, tail_rows, kernel, keeping):
    kernel_taps = kernel.shape[0]
    rows_here = stream.shape[0]
    padded = jnp.concatenate([tail_rows, stream], axis=0).astype(jnp.float32)
    summed = jnp.zeros((rows_here, stream.shape[1]), jnp.float32)
    for offset in range(kernel_taps):
        anchor = kernel_taps - 1 - offset
        summed = (
            summed
            + keeping[offset][:, None]
            * kernel[offset][None, :]
            * padded[anchor : anchor + rows_here]
        )
    return jax.nn.silu(summed).astype(jnp.bfloat16)


def join_states(earlier, later):
    return (earlier[0] * later[0], later[0][:, None, None] * earlier[1] + later[1])


def normalize_rows(hidden, squares, gain_part, row_width):
    return (
        hidden.astype(jnp.float32)
        * lax.rsqrt(squares / row_width + epsilon)[:, None]
        * gain_part[None, :]
    ).astype(jnp.bfloat16)


def pick_logit(logits, target_column):
    columns = jnp.arange(logits.shape[1], dtype=jnp.int32)
    return jnp.sum(jnp.where(columns[None, :] == target_column[:, None], logits, 0.0), axis=1)


def body(
    inner_input,
    gate_input,
    state_inputs,
    step_size,
    resets,
    decay_rate,
    skip_gain,
    conv_inner,
    conv_state,
    norm_gain,
    out_weight,
    residual,
    final_gain,
    head_weight,
    scored,
    targets,
    policy_logprob,
):
    kernel_taps = conv_inner.shape[0]
    rows_here = inner_input.shape[0]
    head_count = step_size.shape[0]
    group_count = state_inputs.shape[2] // STATE
    per_group = head_count // group_count
    margin = kernel_taps - 1
    inner_tail, state_tail, reset_tail = passed_along(
        (
            inner_input[rows_here - margin :],
            state_inputs[:, rows_here - margin :],
            resets[rows_here - margin :].astype(jnp.bfloat16),
        ),
        "ctx",
        1,
    )
    flags = jnp.concatenate([reset_tail.astype(jnp.float32), resets.astype(jnp.float32)])
    counted = jnp.cumsum(flags)
    keeping = jnp.stack(
        [
            (
                counted[margin:] - counted[margin - offset : margin - offset + rows_here] == 0.0
            ).astype(jnp.float32)
            for offset in range(kernel_taps)
        ]
    )
    inner_conv = causal_filter(inner_input, inner_tail, conv_inner, keeping)
    write_map = causal_filter(state_inputs[0], state_tail[0], conv_state[0], keeping)
    read_map = causal_filter(state_inputs[1], state_tail[1], conv_state[1], keeping)
    spans = rows_here // SPAN
    values = inner_conv.reshape(spans, SPAN, head_count, HEAD_DIM)
    writes = write_map.reshape(spans, SPAN, group_count, STATE)
    reads = read_map.reshape(spans, SPAN, group_count, STATE)
    steps_blocked = step_size.reshape(head_count, spans, SPAN).transpose(1, 0, 2)
    cumulated = jnp.cumsum(-decay_rate[None, :, None] * steps_blocked, axis=2)
    segment = jnp.cumsum(resets.reshape(spans, SPAN), axis=1)
    positions = jnp.arange(SPAN)
    causal = (positions[None, :, None] >= positions[None, None, :]) & (
        segment[:, :, None] == segment[:, None, :]
    )
    gaps = cumulated[:, :, :, None] - cumulated[:, :, None, :]
    decay_matrix = jnp.where(causal[:, None], jnp.exp(jnp.where(causal[:, None], gaps, 0.0)), 0.0)
    scores = jnp.einsum("kign,kjgn->kgij", reads, writes, preferred_element_type=jnp.float32)
    mixing = jnp.repeat(scores, per_group, axis=1) * decay_matrix * steps_blocked[:, :, None, :]
    values_wide = values.astype(jnp.float32)
    within = jnp.einsum("khij,kjhp->kihp", mixing, values_wide, precision=precise)
    writes_heads = jnp.repeat(writes, per_group, axis=2).astype(jnp.float32)
    reads_heads = jnp.repeat(reads, per_group, axis=2).astype(jnp.float32)
    to_end = (
        jnp.exp(cumulated[:, :, -1:] - cumulated)
        * (segment[:, None, :] == segment[:, None, -1:])
        * steps_blocked
    )
    weighted = values_wide * to_end.transpose(0, 2, 1)[:, :, :, None]
    span_states = jnp.einsum("kjhp,kjhn->khpn", weighted, writes_heads, precision=precise)
    span_decay = jnp.exp(cumulated[:, :, -1]) * (segment[:, -1] == 0)[:, None]
    from_start = jnp.exp(cumulated) * (segment == 0)[:, None, :]

    def advance(running, item):
        return (item[0][:, None, None] * running + item[1], running)

    empty_state = jnp.zeros((head_count, HEAD_DIM, STATE), jnp.float32)
    device_state, entering = lax.scan(advance, empty_state, (span_decay, span_states))
    decay_prefix = jnp.cumprod(span_decay, axis=0)
    before = jnp.concatenate([jnp.ones((1, head_count), jnp.float32), decay_prefix[:-1]], axis=0)
    incoming = carried_in(
        (decay_prefix[-1], device_state),
        "ctx",
        join_states,
        (jnp.ones((head_count,), jnp.float32), empty_state),
    )
    entering = entering + before[:, :, None, None] * incoming[1][None]
    across = (
        jnp.einsum("kihn,khpn->kihp", reads_heads, entering, precision=precise)
        * from_start.transpose(0, 2, 1)[:, :, :, None]
    )
    mixed_out = (within + across).reshape(rows_here, head_count * HEAD_DIM) + jnp.repeat(
        skip_gain, HEAD_DIM
    )[None, :] * values_wide.reshape(rows_here, head_count * HEAD_DIM)
    gated = mixed_out * jax.nn.silu(gate_input.astype(jnp.float32))
    grouped = gated.reshape(rows_here, group_count, -1)
    inverse_rms = lax.rsqrt(jnp.mean(grouped * grouped, axis=2, keepdims=True) + epsilon)
    normed = ((grouped * inverse_rms).reshape(rows_here, -1) * norm_gain[None, :]).astype(
        jnp.bfloat16
    )
    local_rows = scored - lax.axis_index("ctx") * rows_here
    every_normed = lax.all_gather(normed[local_rows], "ctx", axis=0, tiled=True)
    partial_rows = jnp.dot(every_normed, out_weight, preferred_element_type=jnp.float32)
    summed_rows = lax.psum(partial_rows, "tp")
    returned = lax.all_to_all(summed_rows, "ctx", split_axis=0, concat_axis=1, tiled=True)
    width_part = residual.shape[1]
    own_columns = lax.dynamic_slice_in_dim(
        returned, lax.axis_index("tp") * width_part, width_part, 1
    )
    hidden = (residual[local_rows].astype(jnp.float32) + own_columns).astype(jnp.bfloat16)
    model_width = final_gain.shape[0]
    squares = lax.psum(jnp.sum(jnp.square(hidden.astype(jnp.float32)), axis=1), "tp")
    slice_start = lax.axis_index("tp") * hidden.shape[1]
    payload = normalize_rows(
        hidden,
        squares,
        lax.dynamic_slice_in_dim(final_gain, slice_start, hidden.shape[1]),
        model_width,
    )
    vocab_part = head_weight.shape[1]
    vocab_start = (lax.axis_index("ctx") * lax.axis_size("tp") + lax.axis_index("tp")) * vocab_part
    target_column = targets - vocab_start
    features = lax.all_gather(payload, "tp", axis=1, tiled=True)
    outcome = jnp.dot(
        lax.all_gather(features, "ctx", axis=0, tiled=True),
        head_weight,
        preferred_element_type=jnp.float32,
    )
    row_top = lax.pmax(jnp.max(outcome, axis=1), ("ctx", "tp"))
    summed, picked = lax.psum(
        (jnp.sum(jnp.exp(outcome - row_top[:, None]), axis=1), pick_logit(outcome, target_column)),
        ("ctx", "tp"),
    )
    ref_logprob = picked - row_top - jnp.log(summed)
    token_kl = 0.5 * jnp.square(ref_logprob - policy_logprob)
    return (ref_logprob, token_kl)


def solution(mesh):
    return jax.shard_map(
        body,
        mesh=mesh,
        in_specs=(
            P("ctx", "tp"),
            P("ctx", "tp"),
            P(None, "ctx", "tp"),
            P("tp", "ctx"),
            P("ctx"),
            P("tp"),
            P("tp"),
            P(None, "tp"),
            P(None, None, "tp"),
            P("tp"),
            P("tp", "ctx"),
            P("ctx", "tp"),
            P(),
            P(None, ("ctx", "tp")),
            P("ctx"),
            P(),
            P(),
        ),
        out_specs=(P(), P()),
        check_vma=False,
    )
```

profile of v0, /device:TPU:0, one launch (start us, length us, event | category | flops | bytes accessed | tf_op | source)
XLA Modules:
  0.0 530.9 jit_solution(17188054167340376230)
XLA Ops:
  7.2 0.9 fusion.34
  8.2 2.4 collective-permute-start
  10.6 0.7 slice.169
  11.3 4.5 collective-permute-start.2
  15.8 1.5 slice.156
  17.2 2.5 collective-permute-start.1
  19.8 1.7 slice_bitcast_fusion
  21.4 1.5 fusion.33
  22.9 1.1 fusion.32
  24.0 1.0 reduce_window_sum.39
  25.0 0.6 slice.190
  26.2 0.7 neg.21
  26.9 1.2 compare_convert_fusion
  28.1 0.8 multiply_bitcast_fusion.2
  28.9 0.3 reduce_window_sum.40
  29.2 0.8 slice_reduce_fusion
  30.0 0.5 multiply_multiply_fusion.1
  30.5 0.8 multiply_bitcast_fusion.1
  31.4 0.3 reduce-window.9
  32.2 1.0 maximum_convert_fusion.1
  33.3 1.7 copy_bitcast_fusion
  35.0 1.1 maximum_convert_fusion
  36.1 1.3 copy-done.1
  37.4 2.7 multiply_convert_fusion.1
  40.1 1.6 copy.45
  41.7 1.4 broadcast_in_dim.86
  43.2 3.2 fusion.12
  46.6 0.4 copy-done.53
  47.1 0.7 mul.527
  47.8 20.3 %all-gather.2 = f32[16,1,64]{2,1,0:T(1,128)} all-gather(f32[1,1,64]{2,1,0:T(1,128)S(1)} %reduce-window_bitcast_fusion), channel_id=1, replica_groups=mesh['ctx'=16,'tp'=2] {'ctx'}, dimensions={0}, use_global_device_ids=true | all-gather | bytes 4352 | tf_op jit(solution)/shard_map/all_gather | solution.py:23
  68.1 0.7 compare_select_fusion
  68.7 0.6 pad_clamp_fusion
  69.4 0.6 multiply_bitcast_fusion
  70.1 1.9 fusion.30
  72.2 1.2 fusion
  73.5 0.3 copy_bitcast_fusion.1
  73.8 5.6 %fusion.36 = f32[64,64,128]{2,1,0:T(8,128)} fusion(bf16[128,64,64]{0,2,1:T(8,128)(2,1)S(1)} %bitcast.114, f32[64,128,128]{2,1,0:T(8,128)S(1)} %fusion), kind=kOutput, calls=%fused_computation.99 | convolution fusion | flops 805306368 | bytes 7340032 | tf_op jit(solution)/shard_map/khij,kjhp->kihp/dot_general | solution.py:130
  79.4 136.3 %all-gather.9.cloned.1.call-done = f32[1024,64,128]{2,1,0:T(8,128)} async-done(((f32[64,64,128]{2,1,0:T(8,128)}), f32[1024,64,128]{2,1,0:T(8,128)}) %all-gather.9.cloned.1.call-update) | async-done | bytes 33554448 | tf_op jit(solution)/shard_map/all_gather | solution.py:23
  215.7 1.6 broadcast_in_dim.84
  217.3 0.5 broadcast_in_dim.88
  217.8 1.1 copy-done.3
  218.9 6.5 %fusion.8 = f32[1,128,64,64]{1,3,2,0:T(8,128)} fusion(f32[64,64,128]{2,1,0:T(8,128)} %fusion.36, f32[64,64,128]{2,1,0:T(8,128)S(1)} %copy-done.3, bf16[128,64,128]{2,0,1:T(8,128)(2,1)S(1)} %bitcast.118, f32[128,64]{0,1:T(8,128)S(1)} %copy-done.18), kind=kOutput, calls=%fused_computation.20 | convolution fusion | flops 806354944 | bytes 8421376 | tf_op jit(solution)/shard_map/kihn,khpn->kihp/dot_general | solution.py:158
  225.4 3.0 copy.50
  228.5 6.7 %fusion.31 = f32[128,4096]{1,0:T(8,128)} fusion(bf16[128,4096]{1,0:T(8,128)(2,1)S(1)} %copy-done.6, f32[128,4096]{1,0:T(8,128)} %copy.50, f32[4096]{0:T(1024)S(1)} %copy-done.17, f32[131,4096]{1,0:T(8,128)} %copy-done.1, f32[4096]{0:T(1024)S(1)} %bitcast.130, f32[128]{0:T(128)S(1)} %copy-done.27, f32[4096]{0:T(1024)S(1)} %bitcast.133, f32[128]{0:T(128)S(1)} %copy-done.31, ...), kind=kLoop, calls=%fused_computation.94 | loop fusion | flops 13631488 | bytes 13715456 | tf_op jit(solution)/shard_map/mul | solution.py:166
  235.3 3.7 mul.533
  238.9 1.9 reduce_sum.36
  240.9 0.3 mul.534
  241.3 1.7 copy.55
  243.3 3.3 multiply_convert_fusion
  246.5 2.8 gather_fusion.1
  249.4 105.1 %all-gather.11.cloned.1.call-done = bf16[128,4096]{1,0:T(8,128)(2,1)} async-done(((bf16[8,4096]{1,0:T(8,128)(2,1)}), bf16[128,4096]{1,0:T(8,128)(2,1)}) %all-gather.11.cloned.1.call-update) | async-done | bytes 1048592 | tf_op jit(solution)/shard_map/all_gather | solution.py:171
  354.6 2.3 convolution_bitcast_fusion
  356.9 20.7 %all-reduce.4.cloned.1.call-done = f32[16,8,256]{2,1,0:T(8,128)} async-done(((f32[16,8,256]{2,1,0:T(8,128)}), f32[16,8,256]{2,1,0:T(8,128)}) %all-reduce.4.cloned.1.call-update) | async-done | bytes 131088 | tf_op jit(solution)/shard_map/psum | solution.py:173
  377.6 5.6 %all-to-all-start = ((f32[16,8,256]{2,1,0:T(8,128)}), f32[16,8,256]{2,1,0:T(8,128)S(1)}, u32[]{:S(2)}, u32[]{:S(2)}) async-start(f32[16,8,256]{2,1,0:T(8,128)} %all-reduce.4.cloned.1.call-done), calls=%async_computation | async-start | bytes 262144 | tf_op jit(solution)/shard_map/all_to_all | solution.py:174
  383.3 0.7 gather_fusion
  384.0 7.1 %all-to-all-done = f32[16,8,256]{2,1,0:T(8,128)S(1)} async-done(((f32[16,8,256]{2,1,0:T(8,128)}), f32[16,8,256]{2,1,0:T(8,128)S(1)}, u32[]{:S(2)}, u32[]{:S(2)}) %all-to-all-start) | async-done | bytes 131104 | tf_op jit(solution)/shard_map/all_to_all | solution.py:174
  391.2 4.9 psum.29
  396.2 4.7 all_gather.19
  401.0 34.8 %all-gather.7.cloned.1.call-done = bf16[128,4096]{1,0:T(8,128)(2,1)} async-done(((bf16[8,4096]{1,0:T(8,128)(2,1)}), bf16[128,4096]{1,0:T(8,128)(2,1)}) %all-gather.7.cloned.1.call-update) | async-done | bytes 1048592 | tf_op jit(solution)/shard_map/all_gather | solution.py:194
  435.8 8.5 %fusion.35 = (f32[128]{0:T(128)S(1)}, f32[128,2048]{1,0:T(8,128)S(1)}) fusion(bf16[128,4096]{1,0:T(8,128)(2,1)} %all-gather.7.cloned.1.call-done, bf16[4096,2048]{1,0:T(8,128)(2,1)} %param.32), kind=kOutput, calls=%fused_computation.98 | convolution fusion | flops 2147745792 | bytes 18874880 | tf_op jit(solution)/shard_map/dot_general | solution.py:193
  444.3 38.7 %pmax.7 = f32[128]{0:T(128)S(1)} all-reduce(f32[128]{0:T(128)S(1)} %get-tuple-element.106), channel_id=1, replica_groups=mesh['ctx'=16,'tp'=2] {'ctx','tp'}, use_global_device_ids=true, to_apply=%region_14.15 | all-reduce | flops 128 | bytes 1024 | tf_op jit(solution)/shard_map/pmax | solution.py:198
  483.0 0.4 select_reduce_fusion
  483.5 40.4 %all-reduce.1 = (f32[128]{0:T(128)S(1)}, f32[128]{0:T(128)S(1)}) all-reduce(f32[128]{0:T(128)S(1)} %get-tuple-element.63, f32[128]{0:T(128)S(1)} %get-tuple-element.62), channel_id=1, replica_groups=mesh['ctx'=16,'tp'=2] {'ctx','tp'}, use_global_device_ids=true, to_apply=%region_16.17 | all-reduce | flops 256 | bytes 2048 | tf_op jit(solution)/shard_map/psum | solution.py:199
  523.9 0.5 multiply_multiply_fusion
  (144 shorter events, 1.8 us)
Async XLA Ops:
  7.2 347.4 %copy-start = (bf16[4096,256]{1,0:T(8,128)(2,1)S(1)}, bf16[4096,256]{1,0:T(8,128)(2,1)}, u32[]{:S(2)}) copy-start(bf16[4096,256]{1,0:T(8,128)(2,1)} %param.29) | copy-start | bytes 6291460
  7.2 27.8 %copy-start.7 = (bf16[128,4096]{1,0:T(8,128)(2,1)S(1)}, bf16[128,4096]{1,0:T(8,128)(2,1)}, u32[]{:S(2)}) copy-start(bf16[128,4096]{1,0:T(8,128)(2,1)} %param.19) | copy-start | bytes 3145732
  7.2 208.5 %all-gather.9.cloned.1.call-start = ((), (), s32[]{:S(2)}) async-start(), calls=%async_computation.3 | async-start | bytes 35651584 | tf_op jit(solution)/shard_map/all_gather | solution.py:23
  8.2 23.2 %collective-permute-start = (bf16[3]{0:T(256)(128)(2,1)S(1)}, bf16[3]{0:T(256)(128)(2,1)S(1)}, u32[]{:S(2)}, u32[]{:S(2)}) collective-permute-start(bf16[3]{0:T(256)(128)(2,1)S(1)} %slice.151), channel_id=1, source_target_pairs={{0,2},{2,4},{4,6},{6,8},{8,10},{10,12},{12,14},{14,16},{16,18},{18... | collective-permute-start | bytes 26 | tf_op jit(solution)/shard_map/ppermute | solution.py:18
  11.3 20.9 %collective-permute-start.2 = (bf16[2,3,512]{2,1,0:T(4,128)(2,1)S(1)}, bf16[2,3,512]{2,1,0:T(4,128)(2,1)S(1)}, u32[]{:S(2)}, u32[]{:S(2)}) collective-permute-start(bf16[2,3,512]{2,1,0:T(4,128)(2,1)S(1)} %slice.169), channel_id=1, source_target_pairs={{0,2},{2,4},{4,6},{6,8},{8,10},{10,12},{12,14},{14,16},{16,18},{18... | collective-permute-start | bytes 18440 | tf_op jit(solution)/shard_map/ppermute | solution.py:18
  17.2 17.7 %collective-permute-start.1 = (bf16[3,4096]{1,0:T(4,128)(2,1)}, bf16[3,4096]{1,0:T(4,128)(2,1)}, u32[]{:S(2)}, u32[]{:S(2)}) collective-permute-start(bf16[3,4096]{1,0:T(4,128)(2,1)} %slice.156), channel_id=1, source_target_pairs={{0,2},{2,4},{4,6},{6,8},{8,10},{10,12},{12,14},{14,16},{16,18},{18... | collective-permute-start | bytes 73736 | tf_op jit(solution)/shard_map/ppermute | solution.py:18
  24.0 12.1 %copy-start.9 = (f32[1,4096]{1,0:T(1,128)}, f32[1,4096]{1,0:T(1,128)S(1)}, u32[]{:S(2)}) copy-start(f32[1,4096]{1,0:T(1,128)S(1)} %get-tuple-element.84) | copy-start | bytes 49156
  24.0 12.1 %copy-start.11 = (f32[1,4096]{1,0:T(1,128)}, f32[1,4096]{1,0:T(1,128)S(1)}, u32[]{:S(2)}) copy-start(f32[1,4096]{1,0:T(1,128)S(1)} %get-tuple-element.85) | copy-start | bytes 49156
  24.0 12.1 %copy-start.13 = (f32[1,4096]{1,0:T(1,128)}, f32[1,4096]{1,0:T(1,128)S(1)}, u32[]{:S(2)}) copy-start(f32[1,4096]{1,0:T(1,128)S(1)} %get-tuple-element.86) | copy-start | bytes 49156
  24.0 12.1 %copy-start.15 = (f32[1,4096]{1,0:T(1,128)}, f32[1,4096]{1,0:T(1,128)S(1)}, u32[]{:S(2)}) copy-start(f32[1,4096]{1,0:T(1,128)S(1)} %get-tuple-element.87) | copy-start | bytes 49156
  25.0 1.9 copy-start.49
  32.2 3.9 copy-start.20
  32.2 3.9 copy-start.24
  32.2 3.9 copy-start.28
  32.2 3.9 copy-start.32
  33.3 1.7 copy-start.5
  36.0 1.4 copy-start.1
  40.1 3.0 copy-start.56
  46.4 1.4 copy-start.54
  46.4 22.9 %copy-start.50 = (s32[1,128]{1,0:T(1,128)S(1)}, s32[1,128]{1,0:T(1,128)}, u32[]{:S(2)}) copy-start(s32[1,128]{1,0:T(1,128)} %copy-done.49) | copy-start | bytes 1540
  46.4 23.0 %copy-start.52 = (f32[128]{0:T(128)S(1)}, f32[128]{0:T(128)}, u32[]{:S(2)}) copy-start(f32[128]{0:T(128)} %get-tuple-element.102) | copy-start | bytes 1540
  46.4 23.6 %copy-start.21 = (f32[128]{0:T(128)S(1)}, f32[128]{0:T(128)}, u32[]{:S(2)}) copy-start(f32[128]{0:T(128)} %copy-done.20) | copy-start | bytes 1540
  46.4 23.6 %copy-start.25 = (f32[128]{0:T(128)S(1)}, f32[128]{0:T(128)}, u32[]{:S(2)}) copy-start(f32[128]{0:T(128)} %copy-done.24) | copy-start | bytes 1540
  46.4 23.6 %copy-start.29 = (f32[128]{0:T(128)S(1)}, f32[128]{0:T(128)}, u32[]{:S(2)}) copy-start(f32[128]{0:T(128)} %copy-done.28) | copy-start | bytes 1540
  46.4 23.6 %copy-start.33 = (f32[128]{0:T(128)S(1)}, f32[128]{0:T(128)}, u32[]{:S(2)}) copy-start(f32[128]{0:T(128)} %copy-done.32) | copy-start | bytes 1540
  46.4 23.6 %copy-start.37 = (f32[1,1,512]{2,1,0:T(1,128)S(1)}, f32[1,1,512]{2,1,0:T(1,128)}, u32[]{:S(2)}) copy-start(f32[1,1,512]{2,1,0:T(1,128)} %get-tuple-element.90) | copy-start | bytes 6148
  46.5 23.6 %copy-start.39 = (f32[1,1,512]{2,1,0:T(1,128)S(1)}, f32[1,1,512]{2,1,0:T(1,128)}, u32[]{:S(2)}) copy-start(f32[1,1,512]{2,1,0:T(1,128)} %get-tuple-element.91) | copy-start | bytes 6148
  46.5 23.6 %copy-start.41 = (f32[1,1,512]{2,1,0:T(1,128)S(1)}, f32[1,1,512]{2,1,0:T(1,128)}, u32[]{:S(2)}) copy-start(f32[1,1,512]{2,1,0:T(1,128)} %get-tuple-element.92) | copy-start | bytes 6148
  46.5 23.6 %copy-start.43 = (f32[1,1,512]{2,1,0:T(1,128)S(1)}, f32[1,1,512]{2,1,0:T(1,128)}, u32[]{:S(2)}) copy-start(f32[1,1,512]{2,1,0:T(1,128)} %get-tuple-element.93) | copy-start | bytes 6148
  46.5 23.6 %copy-start.45 = (f32[1,1,512]{2,1,0:T(1,128)S(1)}, f32[1,1,512]{2,1,0:T(1,128)}, u32[]{:S(2)}) copy-start(f32[1,1,512]{2,1,0:T(1,128)} %get-tuple-element.88) | copy-start | bytes 6148
  46.5 23.6 %copy-start.46 = (f32[1,1,512]{2,1,0:T(1,128)S(1)}, f32[1,1,512]{2,1,0:T(1,128)}, u32[]{:S(2)}) copy-start(f32[1,1,512]{2,1,0:T(1,128)} %get-tuple-element.89) | copy-start | bytes 6148
  46.5 23.6 %copy-start.47 = (f32[1,1,512]{2,1,0:T(1,128)S(1)}, f32[1,1,512]{2,1,0:T(1,128)}, u32[]{:S(2)}) copy-start(f32[1,1,512]{2,1,0:T(1,128)} %get-tuple-element.94) | copy-start | bytes 6148
  46.5 23.6 %copy-start.48 = (f32[1,1,512]{2,1,0:T(1,128)S(1)}, f32[1,1,512]{2,1,0:T(1,128)}, u32[]{:S(2)}) copy-start(f32[1,1,512]{2,1,0:T(1,128)} %get-tuple-element.95) | copy-start | bytes 6148
  46.5 308.0 %all-gather.11.cloned.1.call-start = ((), (), s32[]{:S(2)}) async-start(), calls=%async_computation.4 | async-start | bytes 1114112 | tf_op jit(solution)/shard_map/all_gather | solution.py:171
  70.1 2.0 copy-start.8
  72.1 1.3 copy-start.22
  72.1 1.3 copy-start.26
  72.1 1.3 copy-start.30
  72.1 1.3 copy-start.34
  72.1 1.3 copy-start.38
  72.2 1.3 copy-start.40
  72.2 1.3 copy-start.42
  217.3 1.6 copy-start.3
  217.3 1.6 copy-start.18
  225.4 3.1 copy-start.6
  225.4 3.1 copy-start.10
  225.4 3.1 copy-start.12
  225.4 3.1 copy-start.14
  225.4 3.1 copy-start.16
  225.4 3.1 copy-start.17
  225.4 3.1 copy-start.23
  225.4 3.1 copy-start.27
  225.4 3.1 copy-start.31
  225.4 3.1 copy-start.35
  240.9 2.1 copy-start.4
  241.3 2.0 copy-start.2
  241.3 2.0 copy-start.36
  246.5 136.7 %copy-start.19 = (bf16[128,2048]{1,0:T(8,128)(2,1)S(1)}, bf16[128,2048]{1,0:T(8,128)(2,1)}, u32[]{:S(2)}) copy-start(bf16[128,2048]{1,0:T(8,128)(2,1)} %param.30) | copy-start | bytes 1572868
  249.3 134.6 %copy-start.51 = (f32[4096]{0:T(1024)S(1)}, f32[4096]{0:T(1024)}, u32[]{:S(2)}) copy-start(f32[4096]{0:T(1024)} %param.31) | copy-start | bytes 49156
  249.4 151.6 %copy-start.57 = (s32[128]{0:T(128)S(1)}, s32[128]{0:T(128)}, u32[]{:S(2)}) copy-start(s32[128]{0:T(128)} %param.34) | copy-start | bytes 1540
  249.4 128.2 %all-reduce.4.cloned.1.call-start = ((), (), s32[]{:S(2)}) async-start(), calls=%async_computation.1 | async-start | bytes 262144 | tf_op jit(solution)/shard_map/psum | solution.py:173
  377.6 13.5 %all-to-all-start = ((f32[16,8,256]{2,1,0:T(8,128)}), f32[16,8,256]{2,1,0:T(8,128)S(1)}, u32[]{:S(2)}, u32[]{:S(2)}) async-start(f32[16,8,256]{2,1,0:T(8,128)} %all-reduce.4.cloned.1.call-done), calls=%async_computation | async-start | bytes 262144 | tf_op jit(solution)/shard_map/all_to_all | solution.py:174
  383.2 52.6 %all-gather.7.cloned.1.call-start = ((), (), s32[]{:S(2)}) async-start(), calls=%async_computation.2 | async-start | bytes 1114112 | tf_op jit(solution)/shard_map/all_gather | solution.py:194
  401.0 122.9 %copy-start.55 = (f32[128]{0:T(128)S(1)}, f32[128]{0:T(128)}, u32[]{:S(2)}) copy-start(f32[128]{0:T(128)} %param.35) | copy-start | bytes 1540
  (2 other events, 2.0 us)
Sparse Core Ops, SparseCore 0:
  46.7 168.9 all-gather.8
  249.5 105.0 all-gather.10
  357.0 20.4 all-reduce.3
  401.1 34.6 all-gather.6
where the time goes:
time: 533 us; the launch traced here: 531 us
  waiting for transfers between devices  304 us (57%)
  blocking collectives  109 us (20%)
  other arithmetic  30.6 us (6%)
  local copies, waits for them, and re-layouts  28.7 us (5%)
  matrix products  28.1 us (5%)
  between operations  15.3 us (3%)
  starting transfers between devices  15.2 us (3%)
    all_gather x1, waiting for transfers between devices, carried_in(): gathered = jax.tree.map(lambda a: lax.all_gather(a, axis), part)  136 us
    all_gather x1, waiting for transfers between devices, body(): every_normed = lax.all_gather(normed[local_rows], 'ctx', axis=0, tiled=True)  105 us
    psum x1, blocking collectives, body(): lax.psum((jnp.sum(jnp.exp(outcome - row_top[:, None]), axis=1), pick_logi...  40.4 us
    pmax x1, blocking collectives, body(): row_top = lax.pmax(jnp.max(outcome, axis=1), ('ctx', 'tp'))  38.7 us
    all_gather x1, waiting for transfers between devices, body(): lax.all_gather(features, 'ctx', axis=0, tiled=True)  34.8 us
    psum x1, waiting for transfers between devices, body(): summed_rows = lax.psum(partial_rows, 'tp')  20.7 us
    all_gather x1, blocking collectives, carried_in(): gathered = jax.tree.map(lambda a: lax.all_gather(a, axis), part)  20.3 us
  transfers between devices with their start and end apart: 8, of which 5 were waited for; matrix products, arithmetic and copies ran while one was open for 5% of the time, Pallas kernels for 0%

commit v1 on v0

v1 whole, which is shorter than its diff:
```python
import functools
import jax
import jax.numpy as jnp
from jax import lax
from jax.experimental import pallas as pl
from jax.experimental.pallas import tpu as pltpu
from jax.sharding import PartitionSpec as P

HEAD_DIM = 64
STATE = 128
EDGE = 16

epsilon = 1e-05
precise = lax.Precision.HIGHEST
MESH = pl.DeviceIdType.MESH
VMEM = pl.BlockSpec(memory_space=pltpu.VMEM)
ANY = pl.BlockSpec(memory_space=pl.ANY)


def remote(src, dst, send, recv, device):
    return pltpu.make_async_remote_copy(
        src_ref=src, dst_ref=dst, send_sem=send, recv_sem=recv, device_id=device, device_id_type=MESH
    )


def greet(devices):
    barrier = pltpu.get_barrier_semaphore()
    for device in devices:
        pl.semaphore_signal(barrier, inc=1, device_id=device, device_id_type=MESH)
    pl.semaphore_wait(barrier, len(devices))


def spread_kernel(n, tp, q_count, z_count, x_ref, s_ref, d_ref, g_ref, m_ref, r_ref,
                  xo, so, do, go, mo, xh, sh, mh, ro,
                  send, recv, own, edge_send, edge_recv, res_send, res_recv):
    c, t = lax.axis_index("ctx"), lax.axis_index("tp")
    z, q = c // q_count, c % q_count
    total = n * tp
    me = c * tp + t
    barrier = pltpu.get_barrier_semaphore()

    def hello(k, carry):
        other = (me + k) % total
        pl.semaphore_signal(
            barrier, inc=1, device_id=(other // tp, other % tp), device_id_type=MESH
        )
        return carry

    lax.fori_loop(1, total, hello, 0)
    pl.semaphore_wait(barrier, total - 1)
    width = xo.shape[2]
    heads = do.shape[1]
    rows = x_ref.shape[0]

    def cols(ref, k, size):
        return ref.at[:, pl.ds(pl.multiple_of(k * size, 128), size)]

    def parts(k):
        return (
            cols(x_ref, k, width),
            s_ref.at[:, :, pl.ds(pl.multiple_of(k * STATE, 128), STATE)],
            d_ref.at[pl.ds(pl.multiple_of(k * heads, 8), heads), :],
            cols(g_ref, k, width),
            m_ref,
        )

    def slots(k):
        return (xo.at[k], so.at[k], do.at[k], go.at[k], mo.at[k])

    started = []
    tail = pl.ds(rows - EDGE, EDGE)
    next_z = jnp.minimum(z + 1, z_count - 1)

    def edges(k, dst_c):
        wide = pl.ds(pl.multiple_of(k * width, 128), width)
        thin = pl.ds(pl.multiple_of(k * STATE, 128), STATE)
        triple = ((x_ref.at[tail, wide], xh), (s_ref.at[:, tail, thin], sh), (m_ref, mh))
        return [
            remote(a, b, edge_send.at[k, i], edge_recv.at[i], (dst_c, t))
            for i, (a, b) in enumerate(triple)
        ]

    sends_edge = (q == q_count - 1) & (z < z_count - 1)
    gets_edge = z > 0
    if z_count > 1:
        @pl.when(sends_edge)
        def _():
            for k in range(q_count):
                for copy in edges(k, (z + 1) * q_count + k):
                    copy.start()

    for d in range(1, q_count):
        k = (q + d) % q_count
        for i, (a, b) in enumerate(zip(parts(k), slots(q))):
            copy = remote(a, b, send.at[d - 1, i], recv.at[d - 1, i], (z * q_count + k, t))
            copy.start()
            started.append(copy)
    per = n // tp

    def res_copy(j, to_t):
        return remote(
            r_ref.at[j], ro.at[c],
            res_send.at[j * tp + to_t], res_recv.at[c], (t * per + j, to_t)
        )

    for j in range(per):
        for to_t in range(tp):
            mine = (t * per + j == c) & (to_t == t)

            @pl.when(jnp.logical_not(mine))
            def _():
                res_copy(j, to_t).start()

            @pl.when(mine)
            def _():
                pltpu.make_async_copy(r_ref.at[j], ro.at[c], res_recv.at[c]).start()
    locals_ = [
        pltpu.make_async_copy(a, b, own.at[i]) for i, (a, b) in enumerate(zip(parts(q), slots(q)))
    ]
    for copy in locals_:
        copy.start()
    for copy in locals_:
        copy.wait()
    for j in range(per):
        for to_t in range(tp):
            mine = (t * per + j == c) & (to_t == t)

            @pl.when(jnp.logical_not(mine))
            def _():
                res_copy(j, to_t).wait_send()
    for k in range(n):
        pltpu.make_async_copy(ro.at[k], ro.at[k], res_recv.at[k]).wait()
    for copy in started:
        copy.wait_send()
    for d in range(1, q_count):
        k = (q + q_count - d) % q_count
        for i, (a, b) in enumerate(zip(parts(q), slots(k))):
            remote(a, b, send.at[d - 1, i], recv.at[d - 1, i], (z * q_count + k, t)).wait_recv()
    if z_count > 1:
        @pl.when(sends_edge)
        def _():
            for k in range(q_count):
                for copy in edges(k, (z + 1) * q_count + k):
                    copy.wait_send()

        @pl.when(gets_edge)
        def _():
            for i, ref in enumerate((xh, sh, mh)):
                pltpu.make_async_copy(ref, ref, edge_recv.at[i]).wait()


def spread(n, tp, q_count, x, s, d, g, m, r):
    z_count = n // q_count
    rows, all_width = x.shape
    width = all_width // q_count
    heads = d.shape[0] // q_count
    block = r.shape[1] * tp // n
    r = r.reshape(r.shape[0], n // tp, block).transpose(1, 0, 2)
    shape = jax.ShapeDtypeStruct
    outs = (
        shape((q_count, rows, width), x.dtype),
        shape((q_count, 2, rows, STATE), s.dtype),
        shape((q_count, heads, rows), d.dtype),
        shape((q_count, g.shape[0], width), g.dtype),
        shape((q_count,) + m.shape, m.dtype),
        shape((EDGE, width), x.dtype),
        shape((2, EDGE, STATE), s.dtype),
        shape(m.shape, m.dtype),
        shape((n,) + r.shape[1:], r.dtype),
    )
    dma = pltpu.SemaphoreType.DMA
    peers = max(q_count - 1, 1)
    return pl.pallas_call(
        functools.partial(spread_kernel, n, tp, q_count, z_count),
        out_shape=outs,
        in_specs=[ANY, ANY, ANY, VMEM, VMEM, VMEM],
        out_specs=[VMEM] * len(outs),
        scratch_shapes=[
            dma((peers, 5)), dma((peers, 5)), dma((5,)), dma((q_count, 3)), dma((3,)),
            dma((n,)), dma((n,)),
        ],
        compiler_params=pltpu.CompilerParams(collective_id=0, has_side_effects=True),
    )(x, s, d, g, m, r)


def exchange_kernel(stride, size, axis, modes, *refs):
    count = len(modes)
    ins, outs = refs[:count], refs[count : 2 * count]
    send, recv, own = refs[2 * count :]
    me = lax.axis_index(axis)
    place = (me // stride) % size

    def device(k):
        other = me + (k - place) * stride
        c, t = lax.axis_index("ctx"), lax.axis_index("tp")
        return (other, t) if axis == "ctx" else (c, other)

    greet([device((place + d) % size) for d in range(1, size)])

    def source(i, k):
        return ins[i].at[k] if modes[i] else ins[i]

    copies = []
    for d in range(1, size):
        k = (place + d) % size
        for i in range(count):
            copy = remote(
                source(i, k), outs[i].at[place], send.at[d - 1, i], recv.at[d - 1, i], device(k)
            )
            copy.start()
            copies.append(copy)
    for i in range(count):
        pltpu.make_async_copy(source(i, place), outs[i].at[place], own.at[i]).start()
    for i in range(count):
        pltpu.make_async_copy(source(i, place), outs[i].at[place], own.at[i]).wait()
    for copy in copies:
        copy.wait_send()
    for d in range(1, size):
        k = (place + size - d) % size
        for i in range(count):
            remote(
                source(i, place), outs[i].at[k], send.at[d - 1, i], recv.at[d - 1, i], device(k)
            ).wait_recv()


def exchange(arrays, modes, stride, size, axis, ident):
    if size == 1:
        return [a if mode else a[None] for a, mode in zip(arrays, modes)]
    outs = [
        jax.ShapeDtypeStruct(a.shape if mode else (size,) + a.shape, a.dtype)
        for a, mode in zip(arrays, modes)
    ]
    dma = pltpu.SemaphoreType.DMA
    count = len(arrays)
    return pl.pallas_call(
        functools.partial(exchange_kernel, stride, size, axis, modes),
        out_shape=outs,
        in_specs=[VMEM] * count,
        out_specs=[VMEM] * count,
        scratch_shapes=[dma((size - 1, count)), dma((size - 1, count)), dma((count,))],
        compiler_params=pltpu.CompilerParams(collective_id=ident, has_side_effects=True),
    )(*arrays)


def tail_kernel(n, tp, q_count, z_count, n_ref, ow_ref, hw_ref, r_ref, g_ref, t_ref, p_ref, out,
                ow, hw, nrm, both, hid, feat, logit, stat, every,
                own, tp_send, tp_recv, st_send, st_recv, *gather_sems):
    c, t = lax.axis_index("ctx"), lax.axis_index("tp")
    z, q = c // q_count, c % q_count
    total = n * tp
    me = c * tp + t
    get_ow = pltpu.make_async_copy(ow_ref, ow, own.at[0])
    get_hw = pltpu.make_async_copy(hw_ref, hw, own.at[1])
    barrier = pltpu.get_barrier_semaphore()

    def device(k):
        return (k // tp, k % tp)

    def hello(d, carry):
        pl.semaphore_signal(
            barrier, inc=1, device_id=device((me + d) % total), device_id_type=MESH
        )
        return carry

    lax.fori_loop(1, total, hello, 0)
    get_ow.start()
    get_hw.start()
    pl.semaphore_wait(barrier, total - 1)
    core_n = 2 if q_count % 2 == 0 else 1
    x_n = q_count // core_n
    x, core = q // core_n, q % core_n

    def at_x(k):
        return (z * q_count + k * core_n + core, t)

    at_core = (z * q_count + x * core_n + (core_n - 1) - core, t)

    def gathered(slot, mine, sems):
        z_send, z_recv, x_send, x_recv, c_send, c_recv = sems
        sent = []

        def push(copy):
            copy.start()
            sent.append(copy)

        def to_x(ref, dst, d):
            for e in range(1, x_n):
                push(remote(ref, dst, x_send.at[e - 1, d], x_recv.at[e - 1, d], at_x((x + e) % x_n)))

        def to_core(ref, dst, e, d):
            if core_n > 1:
                push(remote(ref, dst, c_send.at[e, d], c_recv.at[e, d], at_core))

        home = slot(q, z)
        for d in range(1, z_count):
            push(remote(mine, home, z_send.at[d], z_recv.at[d], (((z + d) % z_count) * q_count + q, t)))
        to_x(mine, home, 0)
        to_core(mine, home, 0, 0)
        for d in range(z_count):
            k = (z + z_count - d) % z_count
            if d:
                here = slot(q, k)
                remote(here, here, z_send.at[d], z_recv.at[d], at_core).wait_recv()
                to_x(here, here, d)
                to_core(here, here, 0, d)
            for e in range(1, x_n):
                here = slot(((x + x_n - e) % x_n) * core_n + core, k)
                remote(here, here, x_send.at[e - 1, d], x_recv.at[e - 1, d], at_core).wait_recv()
                to_core(here, here, e, d)
        if core_n > 1:
            for d in range(z_count):
                k = (z + z_count - d) % z_count
                for e in range(x_n):
                    here = slot(((x + x_n - e) % x_n) * core_n + 1 - core, k)
                    remote(here, here, c_send.at[e, d], c_recv.at[e, d], at_core).wait_recv()
        return sent

    rows = n_ref.shape[0]
    width = n_ref.shape[1]

    def normed_slot(a, b):
        return nrm.at[a, b]

    pending = gathered(normed_slot, n_ref, gather_sems[:6])
    nrm[q, z] = n_ref[...]
    get_ow.wait()
    partial = jnp.zeros(both.shape[1:], jnp.float32)
    for k in range(q_count):
        partial = partial + jnp.dot(
            nrm[k].reshape(z_count * rows, width),
            ow[k * width : (k + 1) * width, :],
            preferred_element_type=jnp.float32,
        )
    both[t] = partial
    tp_copies = []
    for d in range(1, tp):
        copy = remote(both.at[t], both.at[t], tp_send.at[d], tp_recv.at[d], (c, (t + d) % tp))
        copy.start()
        tp_copies.append(copy)
    for d in range(1, tp):
        here = both.at[(t + tp - d) % tp]
        remote(here, here, tp_send.at[d], tp_recv.at[d], (c, (t + d) % tp)).wait_recv()
    summed = both[0]
    for k in range(1, tp):
        summed = summed + both[k]
    hid[q, z] = (r_ref[...].astype(jnp.float32) + summed).astype(jnp.bfloat16)

    def hidden_slot(a, b):
        return hid.at[a, b]

    pending = pending + tp_copies + gathered(hidden_slot, hid.at[q, z], gather_sems[6:])
    block = hid.shape[3]
    all_rows = hid.shape[2]
    squares = jnp.zeros((all_rows, 1), jnp.float32)
    for k in range(z_count):
        for a in range(q_count):
            piece = hid[a, k].astype(jnp.float32)
            squares = squares + jnp.sum(piece * piece, axis=1, keepdims=True)
    inverse = lax.rsqrt(squares / (n * block) + epsilon)
    for k in range(z_count):
        for a in range(q_count):
            first = (k * q_count + a) * block
            span = slice(first, first + block)
            feat[:, span] = (
                hid[a, k].astype(jnp.float32) * inverse * g_ref[:, span]
            ).astype(jnp.bfloat16)
    get_hw.wait()
    vocab = hw.shape[1]
    tile = min(256, vocab)

    def one_tile(i, carry):
        cols = pl.ds(pl.multiple_of(i * tile, 128), tile)
        logit[:, cols] = jnp.dot(feat[...], hw[:, cols], preferred_element_type=jnp.float32)
        return carry

    lax.fori_loop(0, vocab // tile, one_tile, 0)
    values = logit[...]
    top = jnp.max(values, axis=1, keepdims=True)
    added = jnp.sum(jnp.exp(values - top), axis=1, keepdims=True)
    column = t_ref[...] - me * vocab
    places = lax.broadcasted_iota(jnp.int32, values.shape, 1)
    hit = jnp.sum(jnp.where(places == column, values, 0.0), axis=1, keepdims=True)
    lane = lax.broadcasted_iota(jnp.int32, (all_rows, 128), 1)
    packed = jnp.where(lane == 0, top, jnp.where(lane == 1, added, jnp.where(lane == 2, hit, 0.0)))
    turned = packed.T[:8]
    stat[...] = turned

    def go(d, carry):
        remote(
            stat, every.at[me], st_send.at[d], st_recv.at[d], device((me + d) % total)
        ).start()
        return carry

    lax.fori_loop(1, total, go, 0)
    every[me] = turned

    def done(d, carry):
        here = every.at[(me + total - d) % total]
        copy = remote(stat, here, st_send.at[d], st_recv.at[d], device((me + d) % total))
        copy.wait_send()
        copy.wait_recv()
        return carry

    lax.fori_loop(1, total, done, 0)
    for copy in pending:
        copy.wait_send()
    found = every[...]
    tops = found[:, 0, :]
    row_top = jnp.max(tops, axis=0, keepdims=True)
    full = jnp.sum(found[:, 1, :] * jnp.exp(tops - row_top), axis=0, keepdims=True)
    picked = jnp.sum(found[:, 2, :], axis=0, keepdims=True)
    log_prob = picked - row_top - jnp.log(full)
    out[0:1, :] = log_prob
    out[1:2, :] = 0.5 * jnp.square(log_prob - p_ref[...])


def tail(normed, out_weight, head_weight, res, gain, targets, policy, n, tp, q_count, z_count):
    dma = pltpu.SemaphoreType.DMA
    total = n * tp
    rows, width = normed.shape
    all_rows = z_count * rows
    block = out_weight.shape[1]
    core_n = 2 if q_count % 2 == 0 else 1
    x_n = q_count // core_n
    vmem = pltpu.VMEM
    bf16, f32 = jnp.bfloat16, jnp.float32
    e_n = max(x_n - 1, 1)
    sems = [
        dma((z_count,)), dma((z_count,)), dma((e_n, z_count)), dma((e_n, z_count)),
        dma((x_n, z_count)), dma((x_n, z_count)),
    ]
    result = pl.pallas_call(
        functools.partial(tail_kernel, n, tp, q_count, z_count),
        out_shape=jax.ShapeDtypeStruct((2, all_rows), f32),
        in_specs=[VMEM, ANY, ANY, VMEM, VMEM, VMEM, VMEM],
        out_specs=VMEM,
        scratch_shapes=[
            vmem(out_weight.shape, bf16),
            vmem(head_weight.shape, bf16),
            vmem((q_count, z_count, rows, width), bf16),
            vmem((tp, all_rows, block), f32),
            vmem((q_count, z_count, all_rows, block), bf16),
            vmem((all_rows, n * block), bf16),
            vmem((all_rows, head_weight.shape[1]), f32),
            vmem((8, all_rows), f32),
            vmem((total, 8, all_rows), f32),
            dma((2,)), dma((tp,)), dma((tp,)), dma((total,)), dma((total,)),
        ] + sems + sems,
        compiler_params=pltpu.CompilerParams(
            collective_id=3, has_side_effects=True, vmem_limit_bytes=50 * 1024 * 1024
        ),
    )(normed, out_weight, head_weight, res, gain[None], targets[:, None], policy[None])
    return result[0], result[1]


def causal_filter(stream, tail_rows, kernel, keeping):
    kernel_taps = kernel.shape[0]
    rows_here = stream.shape[0]
    padded = jnp.concatenate([tail_rows, stream], axis=0).astype(jnp.float32)
    summed = jnp.zeros((rows_here, stream.shape[1]), jnp.float32)
    for offset in range(kernel_taps):
        anchor = tail_rows.shape[0] - offset
        summed = (
            summed
            + keeping[offset][:, None]
            * kernel[offset][None, :]
            * padded[anchor : anchor + rows_here]
        )
    return jax.nn.silu(summed).astype(jnp.bfloat16)


def body(
    inner_input,
    gate_input,
    state_inputs,
    step_size,
    resets,
    decay_rate,
    skip_gain,
    conv_inner,
    conv_state,
    norm_gain,
    out_weight,
    residual,
    final_gain,
    head_weight,
    scored,
    targets,
    policy_logprob,
):
    f32 = jnp.float32
    n, tp = lax.axis_size("ctx"), lax.axis_size("tp")
    c, t = lax.axis_index("ctx"), lax.axis_index("tp")
    taps = conv_inner.shape[0]
    rows_here = inner_input.shape[0]
    q_count = state_inputs.shape[2] // STATE
    z_count = n // q_count
    z, q = c // q_count, c % q_count
    picked_rows = scored.shape[0]
    local_rows = scored - c * rows_here
    here = jnp.arange(rows_here, dtype=jnp.int32)
    pick = (local_rows[:, None] == here[None, :]).astype(jnp.bfloat16)
    gate_rows = jnp.dot(pick, gate_input, preferred_element_type=f32).astype(jnp.bfloat16)
    res_rows = jnp.dot(pick, residual, preferred_element_type=f32).astype(jnp.bfloat16)
    meta = jnp.zeros((8, rows_here), f32)
    meta = meta.at[0].set(resets.astype(f32))
    meta = meta.at[1, :picked_rows].set(local_rows.astype(f32))
    xs, ss, ds, gs, ms, x_edge, s_edge, m_edge, res_all = spread(
        n, tp, q_count, inner_input, state_inputs, step_size, gate_rows, meta, res_rows
    )
    tokens = q_count * rows_here
    width = xs.shape[2]
    heads = ds.shape[1]
    rows = q_count * picked_rows
    x_raw = xs.reshape(tokens, width)
    s_raw = ss.transpose(1, 0, 2, 3).reshape(2, tokens, STATE)
    steps = ds.transpose(1, 0, 2).reshape(heads, tokens)
    gate = gs.reshape(rows, width)
    flags = ms[:, 0].reshape(tokens)
    spots = ms[:, 1, :picked_rows] + (jnp.arange(q_count) * rows_here).astype(f32)[:, None]
    spots = spots.reshape(rows).astype(jnp.int32)
    has_edge = z > 0
    margin = taps - 1
    x_tail = jnp.where(has_edge, x_edge[EDGE - margin :], jnp.zeros((), x_edge.dtype))
    s_tail = jnp.where(has_edge, s_edge[:, EDGE - margin :], jnp.zeros((), s_edge.dtype))
    f_tail = jnp.where(has_edge, m_edge[0, rows_here - margin :], 0.0)
    clear = 1.0 - jnp.concatenate([f_tail, flags])
    keeping = [jnp.ones((tokens,), f32)]
    for offset in range(1, taps):
        keeping.append(keeping[-1] * clear[margin - offset + 1 : margin - offset + 1 + tokens])
    taps_x = lax.dynamic_slice_in_dim(conv_inner, q * width, width, 1)
    taps_s = lax.dynamic_slice_in_dim(conv_state, q * STATE, STATE, 2)
    rate = lax.dynamic_slice_in_dim(decay_rate, q * heads, heads)
    skip = lax.dynamic_slice_in_dim(skip_gain, q * heads, heads)
    gain = lax.dynamic_slice_in_dim(norm_gain, q * width, width)
    reads = causal_filter(s_raw[1], s_tail[1], taps_s[1], keeping)
    order = jnp.arange(tokens, dtype=jnp.int32)
    one_hot = (spots[:, None] == order[None, :]).astype(jnp.bfloat16)
    reads = jnp.dot(one_hot, reads, preferred_element_type=f32).astype(jnp.bfloat16)
    (all_reads,) = exchange([reads], (False,), q_count, z_count, "ctx", 1)
    values = causal_filter(x_raw, x_tail, taps_x, keeping)
    writes = causal_filter(s_raw[0], s_tail[0], taps_s[0], keeping)
    rises = -rate[:, None] * steps
    below = order[:, None] >= order[None, :]
    cumulated = jnp.dot(rises, below.T.astype(f32), precision=precise)
    segment = jnp.dot(below.astype(f32), flags, precision=precise)
    pick_f = one_hot.astype(f32)
    row_cum = jnp.dot(cumulated, pick_f.T, precision=precise)
    row_seg = jnp.dot(pick_f, segment, precision=precise)
    values_wide = values.astype(f32)
    to_end = jnp.exp(cumulated[:, -1:] - cumulated) * (segment == segment[-1])[None, :] * steps
    weighted = (values_wide.reshape(tokens, heads, HEAD_DIM) * to_end.T[:, :, None]).reshape(
        tokens, width
    )
    state = lax.dot_general(
        writes.astype(f32), weighted, (((0,), (0,)), ((), ())), precision=precise
    )
    plane_decay = jnp.exp(cumulated[:, -1]) * (segment[-1] == 0)
    outgoing = jnp.dot(
        all_reads.reshape(z_count * rows, STATE).astype(f32), state, precision=precise
    ).reshape(z_count, rows, width)
    decay_block = jnp.broadcast_to(
        jnp.pad(plane_decay, (0, -heads % 128))[None, :], (8, heads + -heads % 128)
    )
    far, decays = exchange([outgoing, decay_block], (True, False), q_count, z_count, "ctx", 2)
    causal = (spots[:, None] >= order[None, :]) & (row_seg[:, None] == segment[None, :])
    gaps = row_cum[:, :, None] - cumulated[:, None, :]
    decay = jnp.where(causal[None], jnp.exp(jnp.where(causal[None], gaps, 0.0)), 0.0)
    scores = lax.dot_general(
        reads, writes, (((1,), (1,)), ((), ())), preferred_element_type=f32
    )
    mixing = scores[None] * decay * steps[:, None, :]
    within = jnp.einsum(
        "hrj,jhp->rhp",
        mixing,
        values_wide.reshape(tokens, heads, HEAD_DIM),
        precision=precise,
    )
    decays = decays[:, 0, :heads]
    carried = jnp.zeros((rows, heads, HEAD_DIM), f32)
    for k in range(z_count):
        later = carried * decays[k][None, :, None] + far[k].reshape(rows, heads, HEAD_DIM)
        carried = jnp.where(k < z, later, carried)
    from_start = jnp.exp(row_cum) * (row_seg == 0)[None, :]
    own_values = jnp.dot(one_hot, values, preferred_element_type=f32)
    mixed = (
        within
        + carried * from_start.T[:, :, None]
        + skip[None, :, None] * own_values.reshape(rows, heads, HEAD_DIM)
    ).reshape(rows, width)
    gated = mixed * jax.nn.silu(gate.astype(f32))
    inverse_rms = lax.rsqrt(jnp.mean(gated * gated, axis=1, keepdims=True) + epsilon)
    normed = (gated * inverse_rms * gain[None, :]).astype(jnp.bfloat16)
    res = res_all.reshape(z_count * rows, -1)
    return tail(
        normed, out_weight, head_weight, res, final_gain, targets, policy_logprob,
        n, tp, q_count, z_count,
    )


def solution(mesh):
    return jax.shard_map(
        body,
        mesh=mesh,
        in_specs=(
            P("ctx", "tp"),
            P("ctx", "tp"),
            P(None, "ctx", "tp"),
            P("tp", "ctx"),
            P("ctx"),
            P("tp"),
            P("tp"),
            P(None, "tp"),
            P(None, None, "tp"),
            P("tp"),
            P("tp", "ctx"),
            P("ctx", "tp"),
            P(),
            P(None, ("ctx", "tp")),
            P("ctx"),
            P(),
            P(),
        ),
        out_specs=(P(), P()),
        check_vma=False,
    )
```

time: 533 us -> 145 us (0.27)
  waiting for transfers between devices: 304 us -> 0 us
  blocking collectives: 109 us -> 0 us
  Pallas kernels: 0 us -> 100 us
  other arithmetic: 30.6 us -> 12.3 us
  matrix products: 28.1 us -> 12.9 us
  starting transfers between devices: 15.2 us -> 0 us
  between operations: 15.3 us -> 1.82 us
  local copies, waits for them, and re-layouts: 28.7 us -> 16.8 us
    all_gather x3 -> x0, waiting for transfers between devices: 276 us -> none  [the longest x1 136 us: carried_in(): gathered = jax.tree.map(lambda a: lax.all_gather(a, axis), part)]
    pallas_call x0 -> x4, Pallas kernels: none -> 100 us  [the longest x1 50.7 us: tail(): pl.pallas_call(functools.partial(tail_kernel, n, tp, q_count, z_count), o...]
    psum x2 -> x0, blocking collectives: 45.4 us -> none  [the longest x1 40.4 us: body(): lax.psum((jnp.sum(jnp.exp(outcome - row_top[:, None]), axis=1), pick_logi...]
    pmax x1 -> x0, blocking collectives: 38.7 us -> none  [body(): row_top = lax.pmax(jnp.max(outcome, axis=1), ('ctx', 'tp'))]
    all_gather x2 -> x0, blocking collectives: 24.9 us -> none  [the longest x1 20.3 us: carried_in(): gathered = jax.tree.map(lambda a: lax.all_gather(a, axis), part)]
    psum x1 -> x0, waiting for transfers between devices: 20.7 us -> none  [body(): summed_rows = lax.psum(partial_rows, 'tp')]
    dot_general x6 -> x12, matrix products: 28.1 us -> 12.9 us  [the longest x1 3.99 us: body(): jnp.einsum('hrj,jhp->rhp', mixing, values_wide.reshape(tokens, heads, HEA...]
    ppermute x3 -> x0, starting transfers between devices: 9.38 us -> none  [passed_along(): return lax.ppermute(shard, axis, pairs)]
  transfers between devices with their start and end apart: 8 -> 0, of which waited for: 5 -> 0; matrix products, arithmetic and copies ran while one was open for 5% -> 0% of each run, Pallas kernels for 0% -> 0%
where the time goes in v1:
time: 145 us; the launch traced here: 144 us
  Pallas kernels  100 us (69%)
  local copies, waits for them, and re-layouts  16.8 us (12%)
  matrix products  12.9 us (9%)
  other arithmetic  12.3 us (8%)
  between operations  1.82 us (1%)
    pallas_call x1, Pallas kernels, tail(): pl.pallas_call(functools.partial(tail_kernel, n, tp, q_count, z_count), o...  50.7 us
    pallas_call x1, Pallas kernels, spread(): pl.pallas_call(functools.partial(spread_kernel, n, tp, q_count, z_count),...  27.9 us
    pallas_call x2, Pallas kernels, exchange(): pl.pallas_call(functools.partial(exchange_kernel, stride, size, axis, mod...  21.5 us
    dot_general x1, matrix products, body(): jnp.einsum('hrj,jhp->rhp', mixing, values_wide.reshape(tokens, heads, HEA...  3.99 us
    another operation x4, local copies, waits for them, and re-layouts, body(): far[k].reshape(rows, heads, HEAD_DIM)  3.21 us

profile of v1, /device:TPU:0, one launch (start us, length us, event | category | flops | bytes accessed | tf_op | source)
XLA Modules:
  0.0 143.9 jit_solution(10301033470689235293)
XLA Ops:
  0.7 0.7 convert_bitcast_fusion
  1.4 0.5 copy-done
  1.9 0.9 convolution_convert_fusion.g_ref
  2.8 1.9 %convolution_convert_fusion.1 = bf16[8,2048]{1,0:T(8,128)(2,1)} fusion(bf16[128,2048]{1,0:T(8,128)(2,1)} %param.32, s32[8]{0:T(128)S(1)} %get-tuple-element.53), kind=kOutput, calls=%fused_computation.1 | convolution fusion | flops 4211712 | bytes 557088 | tf_op jit(solution)/shard_map/dot_general | solution.py:504
  4.7 0.7 convert_bitcast_fusion.1
  5.4 0.1 scatter.9.m_ref
  5.5 0.6 copy-done.20
  6.0 27.9 %shard_map.176 = (bf16[4,128,1024]{2,1,0:T(8,128)(2,1)}, bf16[4,2,128,128]{3,2,1,0:T(8,128)(2,1)}, f32[4,16,128]{2,1,0:T(8,128)}, bf16[4,8,1024]{2,1,0:T(8,128)(...) custom-call(bf16[128,4096]{1,0:T(8,128)(2,1)} %x_ref.1, ...), custom_call_target="tpu_custom_call" | custom-call | tf_op jit(solution)/shard_map/pallas_call | solution.py:173
  34.0 0.7 slice_select_fusion.1
  34.7 1.0 fusion.60
  35.7 0.1 maximum_convert_fusion.1
  35.8 1.0 fusion.55
  36.8 0.8 fusion.50
  37.5 0.7 slice.212
  38.2 0.1 maximum_subtract_fusion
  38.3 0.1 slice_multiply_fusion.12
  38.4 0.3 multiply_convert_fusion.1
  38.7 0.1 squeeze.30
  38.8 0.1 add.119
  38.9 0.1 add.120
  39.0 0.4 convolution_convert_fusion.2.refs_0_
  39.4 0.8 fusion.61
  40.2 0.1 dynamic-slice_negate_fusion
  40.3 0.5 fusion.11
  40.8 0.2 slice_reduce_fusion
  41.0 0.4 fusion.12
  41.3 0.7 slice.245
  42.0 0.6 compare_convert_fusion.1
  42.7 0.7 multiply_bitcast_fusion
  43.4 1.6 %constant_dynamic-slice_fusion.4 = (f32[1,1024]{1,0:T(1,128)}, f32[1,1024]{1,0:T(1,128)}, f32[1,1024]{1,0:T(1,128)}, f32[1,1024]{1,0:T(1,128)}) fusion(f32[4,4096]{1,0:T(4,128)} %param.28, s32[]{:T(128)} %select_n.83, s32[]{:T(128)S(6)} %add.146, s32[]{:T(128)S(6)} %add.145, s32[]{:T(128)S(6)} %add.147), kind=kLoop, calls=%fused_computation.103 | loop fusion | bytes 32784 | tf_op jit(solution)/shard_map/slice | solution.py:466
  44.9 0.7 slice_select_fusion
  45.6 0.2 copy.29
  45.9 0.5 copy.30
  46.5 0.6 maximum_convert_fusion
  47.1 0.1 copy-done.8
  47.2 2.5 %bitcast_multiply_fusion = (f32[512,1024]{0,1:T(8,128)S(1)}, bf16[512,1024]{0,1:T(8,128)(2,1)S(1)}) fusion(f32[512,16]{0,1:T(8,128)S(1)} %copy-done.8, f32[515,1024]{0,1:T(8,128)S(1)} %maximum_convert_fusion, f32[1024]{0:T(1024)S(1)} %bitcast.140, f32[512]{0:T(512)S(1)} %get-tuple-element.50, f32[1024]{0:T(1024)S(1)} %bitcast.138, ...), kind=kLoop, calls=%fused_computation.9 | loop fusion | flops 8912896 | bytes 11589632 | tf_op jit(solution)/shard_map/mul | solution.py:552
  49.8 1.3 convolution_bitcast_fusion
  51.1 7.2 %shard_map.177 = bf16[4,32,128]{2,1,0:T(8,128)(2,1)} custom-call(bf16[32,128]{1,0:T(8,128)(2,1)} %copy-done.13), custom_call_target="tpu_custom_call" | custom-call | tf_op jit(solution)/shard_map/pallas_call | solution.py:235
  58.3 2.0 %fusion.62.refs_0_ = f32[4,32,1024]{2,1,0:T(8,128)} fusion(bf16[4,32,128]{2,1,0:T(8,128)(2,1)} %shard_map.177, f32[128,1024,1]{1,0,2:T(8,128)S(1)} %convolution_bitcast_fusion), kind=kOutput, calls=%fused_computation.137 | convolution fusion | flops 201326592 | bytes 1081344 | tf_op jit(solution)/shard_map/dot_general | solution.py:559
  60.9 0.6 broadcast_in_dim.41.refs_1_
  61.5 14.3 %shard_map.178 = (f32[4,32,1024]{2,1,0:T(8,128)}, f32[4,8,128]{2,1,0:T(8,128)}) custom-call(f32[4,32,1024]{2,1,0:T(8,128)} %fusion.62.refs_0_, f32[8,128]{1,0:T(8,128)} %broadcast_in_dim.41.refs_1_), custom_call_target="tpu_custom_call" | custom-call | tf_op jit(solution)/shard_map/pallas_call | solution.py:235
  75.8 1.2 fusion.59
  77.0 0.8 reshape_squeeze.16
  77.8 0.8 reshape_squeeze.17
  78.6 0.8 reshape_squeeze.18
  79.4 0.8 reshape_squeeze.19
  80.2 1.3 multiply_bitcast_fusion.2
  81.5 0.4 fusion.37
  81.9 0.8 reshape.231
  82.7 0.2 fusion.38
  82.9 0.2 compare_convert_fusion
  83.1 0.6 multiply_bitcast_fusion.1
  83.8 0.6 dynamic_slice.18
  84.4 0.1 fusion.39
  84.5 0.6 copy_bitcast_fusion
  85.1 0.1 reshape.235
  85.3 4.0 %multiply_reduce_fusion = (f32[32]{0:T(128)}, f32[32,16,64]{2,0,1:T(8,128)S(1)}) fusion(f32[32,16,64]{2,1,0:T(8,128)S(1)} %reshape.235, f32[32,16,64]{2,1,0:T(8,128)} %reshape.231, f32[16]{0:T(128)} %dynamic_slice.18, f32[32,16]{0,1:T(8,128)} %multiply_bitcast_fusion.1, f32[32,16,64]{2,1,0:T(8,128)} %reshape_squeeze.19, f32[16]{0:T(128)} %get-tuple-element.65, ...), kind=kOutput, calls=%fused_computation.57 | convolution fusion | flops 203358176 | bytes 2118084 | tf_op jit(solution)/shard_map/hrj,jhp->rhp/dot_general | solution.py:573
  89.3 0.2 copy.37
  89.4 0.8 reshape.232
  90.2 0.7 add_rsqrt_fusion
  90.9 1.0 fusion.36.n_ref
  91.9 0.8 copy.40.t_ref
  92.7 50.7 %shard_map.179 = f32[2,128]{1,0:T(2,128)S(1)} custom-call(bf16[32,1024]{1,0:T(8,128)(2,1)S(1)} %fusion.36.n_ref, bf16[4096,256]{1,0:T(8,128)(2,1)S(1)} %copy-done.1, bf16[4096,2048]{1,0:T(8,128)(2,1)} %hw_ref.1, bf16[128,256]{1,0:T(8,128)(2,1)S(1)} %bitcast.128, f32[1,4096]{1,0:T(1,128)S(1)} %bitcast.129, s32[128,1]{1,0:T(8,128)S(1)} %copy.40.t_ref, ...), custom_call_target="tpu_custom_call" | custom-call | tf_op jit(solution)/shard_map/pallas_call | solution.py:432
  143.4 0.5 slice_bitcast_fusion.2
  (66 shorter events, 0.2 us)
Async XLA Ops:
  0.6 1.2 copy-start
  5.5 0.6 copy-start.20
  34.0 4.7 %copy-start.27 = (f32[4,8,128]{2,1,0:T(8,128)S(1)}, f32[4,8,128]{2,1,0:T(8,128)}, u32[]{:S(2)}) copy-start(f32[4,8,128]{2,1,0:T(8,128)} %get-tuple-element.40) | copy-start | bytes 49156
  35.8 4.4 %copy-start.28 = (f32[64]{0:T(128)S(1)}, f32[64]{0:T(128)}, u32[]{:S(2)}) copy-start(f32[64]{0:T(128)} %param.26) | copy-start | bytes 772
  35.8 4.5 %copy-start.9 = (f32[4,16,128]{2,1,0:T(8,128)S(1)}, f32[4,16,128]{2,1,0:T(8,128)}, u32[]{:S(2)}) copy-start(f32[4,16,128]{2,1,0:T(8,128)} %get-tuple-element.43) | copy-start | bytes 98308
  38.4 2.6 %copy-start.14 = (f32[512]{0:T(512)}, f32[512]{0:T(512)S(1)}, u32[]{:S(2)}) copy-start(f32[512]{0:T(512)S(1)} %get-tuple-element.76) | copy-start | bytes 6148
  38.7 7.2 %copy-start.6 = (bf16[4,128,1024]{2,1,0:T(8,128)(2,1)S(1)}, bf16[4,128,1024]{2,1,0:T(8,128)(2,1)}, u32[]{:S(2)}) copy-start(bf16[4,128,1024]{2,1,0:T(8,128)(2,1)} %get-tuple-element.38) | copy-start | bytes 3145732
  39.0 6.9 %copy-start.23 = (s32[32]{0:T(128)}, s32[32]{0:T(128)S(1)}, u32[]{:S(2)}) copy-start(s32[32]{0:T(128)S(1)} %add_convert_fusion) | copy-start | bytes 388
  39.4 7.6 %copy-start.13 = (bf16[32,128]{1,0:T(8,128)(2,1)}, bf16[32,128]{1,0:T(8,128)(2,1)S(1)}, u32[]{:S(2)}) copy-start(bf16[32,128]{1,0:T(8,128)(2,1)S(1)} %convolution_convert_fusion.2.refs_0_) | copy-start | bytes 24580
  40.7 4.2 %copy-start.11 = (f32[16,512]{1,0:T(8,128)}, f32[16,512]{1,0:T(8,128)S(1)}, u32[]{:S(2)}) copy-start(f32[16,512]{1,0:T(8,128)S(1)} %fusion.11) | copy-start | bytes 98308
  40.9 4.0 %copy-start.25 = (f32[16]{0:T(128)}, f32[16]{0:T(128)S(1)}, u32[]{:S(2)}) copy-start(f32[16]{0:T(128)S(1)} %slice_reduce_fusion) | copy-start | bytes 196
  41.3 3.6 %copy-start.21 = (f32[1,512]{1,0:T(1,128)}, f32[1,512]{1,0:T(1,128)S(1)}, u32[]{:S(2)}) copy-start(f32[1,512]{1,0:T(1,128)S(1)} %fusion.12) | copy-start | bytes 6148
  46.4 0.8 copy-start.8
  46.4 0.8 copy-start.15
  46.4 0.7 copy-start.16
  46.5 0.7 copy-start.17
  46.5 0.7 copy-start.18
  46.5 0.7 copy-start.19
  49.8 31.7 %copy-start.5 = (bf16[512,1024]{0,1:T(8,128)(2,1)}, bf16[512,1024]{0,1:T(8,128)(2,1)S(1)}, u32[]{:S(2)}) copy-start(bf16[512,1024]{0,1:T(8,128)(2,1)S(1)} %get-tuple-element.49) | copy-start | bytes 3145732
  49.8 11.1 %copy-start.26 = (f32[16]{0:T(128)S(1)}, f32[16]{0:T(128)}, u32[]{:S(2)}) copy-start(f32[16]{0:T(128)} %copy-done.25) | copy-start | bytes 196
  58.3 23.2 %copy-start.24 = (s32[32]{0:T(128)S(1)}, s32[32]{0:T(128)}, u32[]{:S(2)}) copy-start(s32[32]{0:T(128)} %copy-done.23) | copy-start | bytes 388
  75.8 6.9 %copy-start.12 = (f32[16,512]{1,0:T(8,128)S(1)}, f32[16,512]{1,0:T(8,128)}, u32[]{:S(2)}) copy-start(f32[16,512]{1,0:T(8,128)} %copy-done.11) | copy-start | bytes 98308
  75.8 7.1 %copy-start.22 = (f32[1,512]{1,0:T(1,128)S(1)}, f32[1,512]{1,0:T(1,128)}, u32[]{:S(2)}) copy-start(f32[1,512]{1,0:T(1,128)} %copy-done.21) | copy-start | bytes 6148
  75.8 8.0 %copy-start.29 = (f32[64]{0:T(128)S(1)}, f32[64]{0:T(128)}, u32[]{:S(2)}) copy-start(f32[64]{0:T(128)} %param.27) | copy-start | bytes 772
  75.8 8.6 %copy-start.10 = (f32[4,16,128]{2,1,0:T(8,128)S(1)}, f32[4,16,128]{2,1,0:T(8,128)}, u32[]{:S(2)}) copy-start(f32[4,16,128]{2,1,0:T(8,128)} %get-tuple-element.43) | copy-start | bytes 98308
  75.8 9.2 %copy-start.7 = (bf16[4,8,1024]{2,1,0:T(8,128)(2,1)S(1)}, bf16[4,8,1024]{2,1,0:T(8,128)(2,1)}, u32[]{:S(2)}) copy-start(bf16[4,8,1024]{2,1,0:T(8,128)(2,1)} %get-tuple-element.46) | copy-start | bytes 196612
  85.2 5.7 %dynamic-slice-start = ((f32[4096]{0:T(1024)}, s32[]{:T(128)}), f32[1024]{0:T(1024)S(1)}, s32[]{:S(2)}) async-start(f32[4096]{0:T(1024)} %param.30, s32[]{:T(128)} %select_n.83), calls=%async_computation | async-start | bytes 8704 | tf_op jit(solution)/shard_map/dynamic_slice | solution.py:535
  85.2 7.4 %copy-start.1 = (bf16[4096,256]{1,0:T(8,128)(2,1)S(1)}, bf16[4096,256]{1,0:T(8,128)(2,1)}, u32[]{:S(2)}) copy-start(bf16[4096,256]{1,0:T(8,128)(2,1)} %ow_ref.1) | copy-start | bytes 6291460
  85.2 7.4 %copy-start.2 = (bf16[16,8,256]{2,1,0:T(8,128)(2,1)S(1)}, bf16[16,8,256]{2,1,0:T(8,128)(2,1)}, u32[]{:S(2)}) copy-start(bf16[16,8,256]{2,1,0:T(8,128)(2,1)} %get-tuple-element.47) | copy-start | bytes 196612
  85.2 7.4 %copy-start.3 = (f32[4096]{0:T(1024)S(1)}, f32[4096]{0:T(1024)}, u32[]{:S(2)}) copy-start(f32[4096]{0:T(1024)} %param.33) | copy-start | bytes 49156
  85.2 7.4 %copy-start.4 = (f32[128]{0:T(128)S(1)}, f32[128]{0:T(128)}, u32[]{:S(2)}) copy-start(f32[128]{0:T(128)} %param.37) | copy-start | bytes 1540

commit v2 on v1

--- a/solution.py
+++ b/solution.py
@@ -183,63 +183,194 @@
     )(x, s, d, g, m, r)
 
 
-def exchange_kernel(stride, size, axis, modes, *refs):
-    count = len(modes)
-    ins, outs = refs[:count], refs[count : 2 * count]
-    send, recv, own = refs[2 * count :]
-    me = lax.axis_index(axis)
-    place = (me // stride) % size
-
-    def device(k):
-        other = me + (k - place) * stride
-        c, t = lax.axis_index("ctx"), lax.axis_index("tp")
-        return (other, t) if axis == "ctx" else (c, other)
-
-    greet([device((place + d) % size) for d in range(1, size)])
-
-    def source(i, k):
-        return ins[i].at[k] if modes[i] else ins[i]
-
-    copies = []
-    for d in range(1, size):
-        k = (place + d) % size
-        for i in range(count):
-            copy = remote(
-                source(i, k), outs[i].at[place], send.at[d - 1, i], recv.at[d - 1, i], device(k)
+def mid_kernel(q_count, z_count, x_ref, xe_ref, s_ref, se_ref, k_ref, d_ref, f_ref, spot_ref,
+               gate_ref, tx_ref, ts_ref, rate_ref, skip_ref, gain_ref, out,
+               pad_x, pad_s, values, writes, reads, mine_r, all_r, y, far, pd, far_pd, mixed, carried,
+               r_send, r_recv, y_send, y_recv, p_send, p_recv):
+    f32, bf16 = jnp.float32, jnp.bfloat16
+    c, t = lax.axis_index("ctx"), lax.axis_index("tp")
+    z, q = c // q_count, c % q_count
+    barrier = pltpu.get_barrier_semaphore()
+
+    def peer(d):
+        return (((z + d) % z_count) * q_count + q, t)
+
+    for d in range(1, z_count):
+        pl.semaphore_signal(barrier, inc=1, device_id=peer(d), device_id_type=MESH)
+    tokens, width = values.shape
+    piece = tokens // q_count
+    heads = d_ref.shape[0]
+    rows = mine_r.shape[0]
+    taps = tx_ref.shape[0]
+    has_edge = (z > 0).astype(f32)
+    keep = k_ref[...].T
+
+    def filtered(pad, kernel, start, target):
+        total = jnp.zeros((piece, pad.shape[1]), f32)
+        for off in range(taps):
+            total = total + (
+                keep[start : start + piece, off : off + 1]
+                * kernel[off : off + 1]
+                * pad[EDGE - off + start : EDGE - off + start + piece, :]
             )
-            copy.start()
-            copies.append(copy)
-    for i in range(count):
-        pltpu.make_async_copy(source(i, place), outs[i].at[place], own.at[i]).start()
-    for i in range(count):
-        pltpu.make_async_copy(source(i, place), outs[i].at[place], own.at[i]).wait()
-    for copy in copies:
+        target[start : start + piece, :] = jax.nn.silu(total).astype(bf16)
+
+    thin = pl.ds(pl.multiple_of(q * STATE, 128), STATE)
+    for which, target in ((1, reads), (0, writes)):
+        edge = se_ref[which].astype(f32)
+        pad_s[:EDGE, :] = jnp.where(has_edge > 0.0, edge, 0.0)
+        for k in range(q_count):
+            pad_s[EDGE + k * piece : EDGE + (k + 1) * piece, :] = s_ref[k, which].astype(f32)
+        kernel = ts_ref[which, :, thin]
+        for k in range(q_count):
+            filtered(pad_s, kernel, k * piece, target)
+    spots = spot_ref[...]
+    lanes = lax.broadcasted_iota(jnp.int32, (rows, tokens), 1)
+    pick_f = jnp.where(spots == lanes, 1.0, 0.0)
+    pick = pick_f.astype(bf16)
+    mine_r[...] = jnp.dot(pick, reads[...], preferred_element_type=f32).astype(bf16)
+    pl.semaphore_wait(barrier, z_count - 1)
+    sent = []
+    for d in range(1, z_count):
+        copy = remote(mine_r, all_r.at[z], r_send.at[d], r_recv.at[d], peer(d))
+        copy.start()
+        sent.append(copy)
+    all_r[z] = mine_r[...]
+    wide = pl.ds(pl.multiple_of(q * width, 128), width)
+    kernel_x = tx_ref[:, wide]
+    pad_x[:EDGE, :] = jnp.where(has_edge > 0.0, xe_ref[...].astype(f32), 0.0)
+    for k in range(q_count):
+        pad_x[EDGE + k * piece : EDGE + (k + 1) * piece, :] = x_ref[k].astype(f32)
+    for k in range(q_count):
+        filtered(pad_x, kernel_x, k * piece, values)
+    steps = d_ref[...]
+    lower = jnp.where(
+        lax.broadcasted_iota(jnp.int32, (tokens, tokens), 0)
+        <= lax.broadcasted_iota(jnp.int32, (tokens, tokens), 1),
+        1.0, 0.0,
+    )
+    runs = jnp.concatenate([-rate_ref[q] * steps, f_ref[...]], axis=0)
+    sums = jnp.dot(runs, lower, precision=precise, preferred_element_type=f32)
+    cumulated = sums[:heads]
+    segment = sums[heads : heads + 1]
+    at_rows = lax.dot_general(
+        pick_f, sums, (((1,), (1,)), ((), ())), precision=precise, preferred_element_type=f32
+    )
+    row_cum = at_rows[:, :heads]
+    row_seg = at_rows[:, heads : heads + 1]
+    last = cumulated[:, tokens - 1 : tokens]
+    last_seg = segment[:, tokens - 1 : tokens]
+    to_end = jnp.exp(last - cumulated) * jnp.where(segment == last_seg, 1.0, 0.0) * steps
+    spread_heads = jnp.where(
+        lax.broadcasted_iota(jnp.int32, (heads, width), 0)
+        == lax.broadcasted_iota(jnp.int32, (heads, width), 1) // HEAD_DIM,
+        1.0, 0.0,
+    )
+
+    def widen(a):
+        return jnp.dot(a, spread_heads, precision=precise, preferred_element_type=f32)
+
+    plane = jnp.broadcast_to(jnp.exp(last) * jnp.where(last_seg == 0.0, 1.0, 0.0), (heads, 128))
+    pd[...] = widen(plane.T[:8])
+    weighted = values[...].astype(f32) * widen(to_end.T)
+    state = jnp.dot(
+        writes[...].astype(f32).T, weighted, precision=precise, preferred_element_type=f32
+    )
+    for d in range(1, z_count):
+        here = all_r.at[(z + z_count - d) % z_count]
+        remote(mine_r, here, r_send.at[d], r_recv.at[d], peer(d)).wait_recv()
+    for k in range(z_count):
+        y[k] = jnp.dot(
+            all_r[k].astype(f32), state, precision=precise, preferred_element_type=f32
+        )
+
+    def outgoing(d):
+        return (
+            remote(y.at[(z + d) % z_count], far.at[z], y_send.at[d], y_recv.at[d], peer(d)),
+            remote(pd, far_pd.at[z], p_send.at[d], p_recv.at[d], peer(d)),
+        )
+
+    for d in range(1, z_count):
+        @pl.when(z + d < z_count)
+        def _():
+            for copy in outgoing(d):
+                copy.start()
+    scores = lax.dot_general(
+        mine_r[...], writes[...], (((1,), (1,)), ((), ())), preferred_element_type=f32
+    )
+    causal = (spots >= lanes) & (row_seg == segment)
+    half = lax.broadcasted_iota(jnp.int32, (rows, 2 * HEAD_DIM), 1) < HEAD_DIM
+    for pair in range(heads // 2):
+        mixes = []
+        for h in (2 * pair, 2 * pair + 1):
+            gaps = row_cum[:, h : h + 1] - cumulated[h : h + 1]
+            decay = jnp.where(causal, jnp.exp(jnp.where(causal, gaps, 0.0)), 0.0)
+            mixes.append(scores * decay * steps[h : h + 1])
+        span = slice(pair * 2 * HEAD_DIM, (pair + 1) * 2 * HEAD_DIM)
+        product = jnp.dot(
+            jnp.concatenate(mixes, axis=0), values[:, span].astype(f32),
+            precision=precise, preferred_element_type=f32,
+        )
+        mixed[:, span] = jnp.where(half, product[:rows], product[rows:])
+    own_values = jnp.dot(pick, values[...], preferred_element_type=f32)
+    from_start = jnp.exp(row_cum) * jnp.where(row_seg == 0.0, 1.0, 0.0)
+    factors = widen(
+        jnp.concatenate([from_start, jnp.broadcast_to(skip_ref[q], (8, heads))], axis=0)
+    )
+    gate = jax.nn.silu(gate_ref[...].astype(f32))
+    carried[...] = jnp.zeros((rows, width), f32)
+    for d in range(z_count - 1, 0, -1):
+        @pl.when(z - d >= 0)
+        def _():
+            k = z - d + jnp.where(z - d < 0, z_count, 0)
+            here, there = far.at[k], far_pd.at[k]
+            remote(here, here, y_send.at[d], y_recv.at[d], peer(d)).wait_recv()
+            remote(there, there, p_send.at[d], p_recv.at[d], peer(d)).wait_recv()
+            carried[...] = carried[...] * far_pd[k][0:1] + far[k]
+    gated = (
+        mixed[...] + carried[...] * factors[:rows] + factors[rows : rows + 1] * own_values
+    ) * gate
+    scale = lax.rsqrt(jnp.mean(gated * gated, axis=1, keepdims=True) + epsilon)
+    out[...] = (gated * scale * gain_ref[:, wide]).astype(bf16)
+    for copy in sent:
         copy.wait_send()
-    for d in range(1, size):
-        k = (place + size - d) % size
-        for i in range(count):
-            remote(
-                source(i, place), outs[i].at[k], send.at[d - 1, i], recv.at[d - 1, i], device(k)
-            ).wait_recv()
-
-
-def exchange(arrays, modes, stride, size, axis, ident):
-    if size == 1:
-        return [a if mode else a[None] for a, mode in zip(arrays, modes)]
-    outs = [
-        jax.ShapeDtypeStruct(a.shape if mode else (size,) + a.shape, a.dtype)
-        for a, mode in zip(arrays, modes)
-    ]
-    dma = pltpu.SemaphoreType.DMA
-    count = len(arrays)
+    for d in range(1, z_count):
+        @pl.when(z + d < z_count)
+        def _():
+            for copy in outgoing(d):
+                copy.wait_send()
+
+
+def middle(xs, x_edge, ss, s_edge, keeps, steps, flags, spots, gate, taps_x, taps_s, rate, skip, gain,
+           q_count, z_count):
+    f32, bf16 = jnp.float32, jnp.bfloat16
+    tokens = steps.shape[1]
+    rows, width = gate.shape
+    dma, vmem = pltpu.SemaphoreType.DMA, pltpu.VMEM
     return pl.pallas_call(
-        functools.partial(exchange_kernel, stride, size, axis, modes),
-        out_shape=outs,
-        in_specs=[VMEM] * count,
-        out_specs=[VMEM] * count,
-        scratch_shapes=[dma((size - 1, count)), dma((size - 1, count)), dma((count,))],
-        compiler_params=pltpu.CompilerParams(collective_id=ident, has_side_effects=True),
-    )(*arrays)
+        functools.partial(mid_kernel, q_count, z_count),
+        out_shape=jax.ShapeDtypeStruct((rows, width), bf16),
+        in_specs=[VMEM] * 14,
+        out_specs=VMEM,
+        scratch_shapes=[
+            vmem((EDGE + tokens, width), f32),
+            vmem((EDGE + tokens, STATE), f32),
+            vmem((tokens, width), bf16),
+            vmem((tokens, STATE), bf16),
+            vmem((tokens, STATE), bf16),
+            vmem((rows, STATE), bf16),
+            vmem((z_count, rows, STATE), bf16),
+            vmem((z_count, rows, width), f32),
+            vmem((z_count, rows, width), f32),
+            vmem((8, width), f32),
+            vmem((z_count, 8, width), f32),
+            vmem((rows, width), f32),
+            vmem((rows, width), f32),
+        ] + [dma((z_count,))] * 6,
+        compiler_params=pltpu.CompilerParams(
+            collective_id=1, has_side_effects=True, vmem_limit_bytes=50 * 1024 * 1024
+        ),
+    )(xs, x_edge, ss, s_edge, keeps, steps, flags, spots, gate, taps_x, taps_s, rate, skip, gain)
 
 
 def tail_kernel(n, tp, q_count, z_count, n_ref, ow_ref, hw_ref, r_ref, g_ref, t_ref, p_ref, out,
@@ -451,22 +582,6 @@
         ),
     )(normed, out_weight, head_weight, res, gain[None], targets[:, None], policy[None])
     return result[0], result[1]
-
-
-def causal_filter(stream, tail_rows, kernel, keeping):
-    kernel_taps = kernel.shape[0]
-    rows_here = stream.shape[0]
-    padded = jnp.concatenate([tail_rows, stream], axis=0).astype(jnp.float32)
-    summed = jnp.zeros((rows_here, stream.shape[1]), jnp.float32)
-    for offset in range(kernel_taps):
-        anchor = tail_rows.shape[0] - offset
-        summed = (
-            summed
-            + keeping[offset][:, None]
-            * kernel[offset][None, :]
-            * padded[anchor : anchor + rows_here]
-        )
-    return jax.nn.silu(summed).astype(jnp.bfloat16)
 
 
 def body(
@@ -512,85 +627,23 @@
     width = xs.shape[2]
     heads = ds.shape[1]
     rows = q_count * picked_rows
-    x_raw = xs.reshape(tokens, width)
-    s_raw = ss.transpose(1, 0, 2, 3).reshape(2, tokens, STATE)
     steps = ds.transpose(1, 0, 2).reshape(heads, tokens)
     gate = gs.reshape(rows, width)
     flags = ms[:, 0].reshape(tokens)
     spots = ms[:, 1, :picked_rows] + (jnp.arange(q_count) * rows_here).astype(f32)[:, None]
-    spots = spots.reshape(rows).astype(jnp.int32)
-    has_edge = z > 0
+    spots = spots.reshape(rows, 1).astype(jnp.int32)
     margin = taps - 1
-    x_tail = jnp.where(has_edge, x_edge[EDGE - margin :], jnp.zeros((), x_edge.dtype))
-    s_tail = jnp.where(has_edge, s_edge[:, EDGE - margin :], jnp.zeros((), s_edge.dtype))
-    f_tail = jnp.where(has_edge, m_edge[0, rows_here - margin :], 0.0)
+    f_tail = jnp.where(z > 0, m_edge[0, rows_here - margin :], 0.0)
     clear = 1.0 - jnp.concatenate([f_tail, flags])
     keeping = [jnp.ones((tokens,), f32)]
     for offset in range(1, taps):
         keeping.append(keeping[-1] * clear[margin - offset + 1 : margin - offset + 1 + tokens])
-    taps_x = lax.dynamic_slice_in_dim(conv_inner, q * width, width, 1)
-    taps_s = lax.dynamic_slice_in_dim(conv_state, q * STATE, STATE, 2)
-    rate = lax.dynamic_slice_in_dim(decay_rate, q * heads, heads)
-    skip = lax.dynamic_slice_in_dim(skip_gain, q * heads, heads)
-    gain = lax.dynamic_slice_in_dim(norm_gain, q * width, width)
-    reads = causal_filter(s_raw[1], s_tail[1], taps_s[1], keeping)
-    order = jnp.arange(tokens, dtype=jnp.int32)
-    one_hot = (spots[:, None] == order[None, :]).astype(jnp.bfloat16)
-    reads = jnp.dot(one_hot, reads, preferred_element_type=f32).astype(jnp.bfloat16)
-    (all_reads,) = exchange([reads], (False,), q_count, z_count, "ctx", 1)
-    values = causal_filter(x_raw, x_tail, taps_x, keeping)
-    writes = causal_filter(s_raw[0], s_tail[0], taps_s[0], keeping)
-    rises = -rate[:, None] * steps
-    below = order[:, None] >= order[None, :]
-    cumulated = jnp.dot(rises, below.T.astype(f32), precision=precise)
-    segment = jnp.dot(below.astype(f32), flags, precision=precise)
-    pick_f = one_hot.astype(f32)
-    row_cum = jnp.dot(cumulated, pick_f.T, precision=precise)
-    row_seg = jnp.dot(pick_f, segment, precision=precise)
-    values_wide = values.astype(f32)
-    to_end = jnp.exp(cumulated[:, -1:] - cumulated) * (segment == segment[-1])[None, :] * steps
-    weighted = (values_wide.reshape(tokens, heads, HEAD_DIM) * to_end.T[:, :, None]).reshape(
-        tokens, width
-    )
-    state = lax.dot_general(
-        writes.astype(f32), weighted, (((0,), (0,)), ((), ())), precision=precise
-    )
-    plane_decay = jnp.exp(cumulated[:, -1]) * (segment[-1] == 0)
-    outgoing = jnp.dot(
-        all_reads.reshape(z_count * rows, STATE).astype(f32), state, precision=precise
-    ).reshape(z_count, rows, width)
-    decay_block = jnp.broadcast_to(
-        jnp.pad(plane_decay, (0, -heads % 128))[None, :], (8, heads + -heads % 128)
-    )
-    far, decays = exchange([outgoing, decay_block], (True, False), q_count, z_count, "ctx", 2)
-    causal = (spots[:, None] >= order[None, :]) & (row_seg[:, None] == segment[None, :])
-    gaps = row_cum[:, :, None] - cumulated[:, None, :]
-    decay = jnp.where(causal[None], jnp.exp(jnp.where(causal[None], gaps, 0.0)), 0.0)
-    scores = lax.dot_general(
-        reads, writes, (((1,), (1,)), ((), ())), preferred_element_type=f32
-    )
-    mixing = scores[None] * decay * steps[:, None, :]
-    within = jnp.einsum(
-        "hrj,jhp->rhp",
-        mixing,
-        values_wide.reshape(tokens, heads, HEAD_DIM),
-        precision=precise,
-    )
-    decays = decays[:, 0, :heads]
-    carried = jnp.zeros((rows, heads, HEAD_DIM), f32)
-    for k in range(z_count):
-        later = carried * decays[k][None, :, None] + far[k].reshape(rows, heads, HEAD_DIM)
-        carried = jnp.where(k < z, later, carried)
-    from_start = jnp.exp(row_cum) * (row_seg == 0)[None, :]
-    own_values = jnp.dot(one_hot, values, preferred_element_type=f32)
-    mixed = (
-        within
-        + carried * from_start.T[:, :, None]
-        + skip[None, :, None] * own_values.reshape(rows, heads, HEAD_DIM)
-    ).reshape(rows, width)
-    gated = mixed * jax.nn.silu(gate.astype(f32))
-    inverse_rms = lax.rsqrt(jnp.mean(gated * gated, axis=1, keepdims=True) + epsilon)
-    normed = (gated * inverse_rms * gain[None, :]).astype(jnp.bfloat16)
+    keeps = jnp.pad(jnp.stack(keeping), ((0, -taps % 8), (0, 0)))
+    normed = middle(
+        xs, x_edge, ss, s_edge, keeps, steps, jnp.broadcast_to(flags[None], (8, tokens)), spots, gate,
+        conv_inner, conv_state, decay_rate.reshape(q_count, heads, 1),
+        skip_gain.reshape(q_count, 1, heads), norm_gain[None], q_count, z_count,
+    )
     res = res_all.reshape(z_count * rows, -1)
     return tail(
         normed, out_weight, head_weight, res, final_gain, targets, policy_logprob,

time: 145 us -> 126 us (0.87)
  matrix products: 12.9 us -> 2.8 us
  other arithmetic: 12.3 us -> 2.4 us
  Pallas kernels: 100 us -> 102 us
    unnamed x60 -> x28, local copies, waits for them, and re-layouts: 1.31 us -> 11.6 us
    dot_general x10 -> x0, matrix products: 10.1 us -> none  [the longest x1 3.99 us: body(): jnp.einsum('hrj,jhp->rhp', mixing, values_wide.reshape(tokens, heads, HEA...]
    pallas_call x1, Pallas kernels: 50.7 us -> 56.1 us  [tail(): pl.pallas_call(functools.partial(tail_kernel, n, tp, q_count, z_count), o...]
    slice x5 -> x0, local copies, waits for them, and re-layouts: 4.56 us -> none  [the longest x1 1.55 us: causal_filter(): kernel[offset][None, :]]
    another operation x4 -> x1, local copies, waits for them, and re-layouts: 3.21 us -> 0.01 us  [body(): keeps = jnp.pad(jnp.stack(keeping), ((0, -taps % 8), (0, 0)))]
    mul x3 -> x0, other arithmetic: 3.18 us -> none  [the longest x1 2.54 us: body(): values_wide.reshape(tokens, heads, HEAD_DIM) * to_end.T[:, :, None]]
    pallas_call x2 -> x1, Pallas kernels: 21.5 us -> 18.4 us  [middle(): pl.pallas_call(functools.partial(mid_kernel, q_count, z_count), out_shape...]
    convert_element_type x6 -> x1, other arithmetic: 2.55 us -> 0.01 us  [body(): spots = spots.reshape(rows, 1).astype(jnp.int32)]
where the time goes in v2:
time: 126 us; the launch traced here: 125 us
  Pallas kernels  102 us (81%)
  local copies, waits for them, and re-layouts  17.1 us (14%)
  matrix products  2.8 us (2%)
  other arithmetic  2.4 us (2%)
    pallas_call x1, Pallas kernels, tail(): pl.pallas_call(functools.partial(tail_kernel, n, tp, q_count, z_count), o...  56.1 us
    pallas_call x1, Pallas kernels, spread(): pl.pallas_call(functools.partial(spread_kernel, n, tp, q_count, z_count),...  27.9 us
    pallas_call x1, Pallas kernels, middle(): pl.pallas_call(functools.partial(mid_kernel, q_count, z_count), out_shape...  18.4 us
    unnamed x28, local copies, waits for them, and re-layouts  11.6 us

profile of v2, /device:TPU:0, one launch (start us, length us, event | category | flops | bytes accessed | tf_op | source)
XLA Modules:
  0.0 125.4 jit_solution(7486593868221921948)
XLA Ops:
  0.6 0.0 copy-start
  0.7 0.7 convert_bitcast_fusion
  1.4 0.5 copy-done
  1.9 0.9 convolution_convert_fusion.g_ref
  2.8 1.9 %convolution_convert_fusion.1 = bf16[8,2048]{1,0:T(8,128)(2,1)} fusion(bf16[128,2048]{1,0:T(8,128)(2,1)} %param.32, s32[8]{0:T(128)S(1)} %get-tuple-element.47), kind=kOutput, calls=%fused_computation.1 | convolution fusion | flops 4211712 | bytes 557088 | tf_op jit(solution)/shard_map/dot_general | solution.py:619
  4.7 0.7 convert_bitcast_fusion.1
  5.3 0.1 scatter.9.m_ref
  5.4 0.0 copy-start.13
  5.4 0.6 copy-done.13
  6.0 27.9 %shard_map.176 = (bf16[4,128,1024]{2,1,0:T(8,128)(2,1)}, bf16[4,2,128,128]{3,2,1,0:T(8,128)(2,1)}, f32[4,16,128]{2,1,0:T(8,128)}, bf16[4,8,1024]{2,1,0:T(8,128)(...) custom-call(bf16[128,4096]{1,0:T(8,128)(2,1)} %x_ref.1, ...), custom_call_target="tpu_custom_call" | custom-call | tf_op jit(solution)/shard_map/pallas_call | solution.py:173
  34.0 0.8 fusion.2
  34.7 0.7 slice.58
  35.4 0.1 maximum_subtract_fusion
  35.5 0.1 slice_multiply_fusion
  35.6 0.1 pad_maximum_fusion
  35.7 0.7 slice_reduce_fusion
  36.4 0.1 squeeze.10
  36.5 0.1 add.27
  36.6 0.1 add.28
  36.7 0.1 copy.26
  36.8 0.8 copy_bitcast_fusion.d_ref
  37.5 0.8 reshape.122.rate_ref
  38.3 0.7 reshape.120
  39.1 0.0 copy-start.2
  39.1 1.2 copy-done.2
  40.3 0.0 copy-start.3
  40.3 0.9 copy-done.3
  41.2 0.0 copy-start.5
  41.2 0.8 copy-done.5
  42.1 0.0 copy-start.6
  42.1 0.8 copy-done.6
  42.9 0.0 copy-start.7
  42.9 0.8 copy-done.7
  43.7 0.0 copy-start.8
  43.7 0.7 copy-done.8
  44.4 0.0 copy-start.9
  44.4 0.7 copy-done.9
  45.1 0.0 copy-start.11
  45.1 0.7 copy-done.11
  45.8 18.4 %shard_map.177.n_ref = bf16[32,1024]{1,0:T(8,128)(2,1)S(1)} custom-call(bf16[4,128,1024]{2,1,0:T(8,128)(2,1)S(1)} %copy-done.2, bf16[16,1024]{1,0:T(8,128)(2,1)S(1)} %copy-done.7, bf16[4,2,128,128]{3,2,1,0:T(8,128)(2,1)S(1)} %copy-done.3, bf16[2,16,128]{2,1,0:T(8,128)(2,1)S(1)} %copy-done.11, f32[8,512]{1,0:T(8,128)S(1)} %pad.10.k_ref, ...), custom_call_target="tpu_custom_call" | custom-call | tf_op jit(solution)/shard_map/pallas_call | solution.py:350
  64.2 0.8 copy.29.t_ref
  64.9 0.0 copy-start.1
  65.0 1.6 %copy-done.1 = bf16[4096,256]{1,0:T(8,128)(2,1)S(1)} copy-done((bf16[4096,256]{1,0:T(8,128)(2,1)S(1)}, bf16[4096,256]{1,0:T(8,128)(2,1)}, u32[]{:S(2)}) %copy-start.1) | copy-done | bytes 2097176
  66.5 0.0 copy-start.4
  66.5 0.8 copy-done.4
  67.4 0.0 copy-start.10
  67.4 0.7 copy-done.10
  68.1 0.0 copy-start.12
  68.1 0.7 copy-done.12
  68.8 56.1 %shard_map.178 = f32[2,128]{1,0:T(2,128)S(1)} custom-call(bf16[32,1024]{1,0:T(8,128)(2,1)S(1)} %shard_map.177.n_ref, bf16[4096,256]{1,0:T(8,128)(2,1)S(1)} %copy-done.1, bf16[4096,2048]{1,0:T(8,128)(2,1)} %hw_ref.1, bf16[128,256]{1,0:T(8,128)(2,1)S(1)} %bitcast.33, f32[1,4096]{1,0:T(1,128)S(1)} %bitcast.36, s32[128,1]{1,0:T(8,128)S(1)} %copy.29.t_ref, ...), custom_call_target="tpu_custom_call" | custom-call | tf_op jit(solution)/shard_map/pallas_call | solution.py:563
  124.8 0.5 slice_bitcast_fusion
  (7 shorter events, 0.0 us)
Async XLA Ops:
  0.6 1.2 copy-start
  5.4 0.6 copy-start.13
  39.1 1.2 copy-start.2
  40.3 0.9 copy-start.3
  41.2 0.8 copy-start.5
  42.1 0.8 copy-start.6
  42.9 0.8 copy-start.7
  43.7 0.7 copy-start.8
  44.4 0.7 copy-start.9
  45.1 0.7 copy-start.11
  64.9 1.6 %copy-start.1 = (bf16[4096,256]{1,0:T(8,128)(2,1)S(1)}, bf16[4096,256]{1,0:T(8,128)(2,1)}, u32[]{:S(2)}) copy-start(bf16[4096,256]{1,0:T(8,128)(2,1)} %ow_ref.1) | copy-start | bytes 6291460
  66.5 0.8 copy-start.4
  67.4 0.7 copy-start.10
  68.1 0.7 copy-start.12

commit v3 on v2

--- a/solution.py
+++ b/solution.py
@@ -183,6 +183,30 @@
     )(x, s, d, g, m, r)
 
 
+def staged(kernel, skip, count, shapes):
+    def run(*refs):
+        ins, rest, held, sems = (
+            refs[:count], refs[count : -len(shapes) - 1], refs[-len(shapes) - 1 : -1], refs[-1]
+        )
+        held = iter(held)
+        views, copies = [], []
+        for i, ref in enumerate(ins):
+            if i in skip:
+                views.append(ref)
+                continue
+            local = next(held)
+            copy = pltpu.make_async_copy(ref, local, sems.at[len(copies)])
+            copy.start()
+            copies.append(copy)
+            views.append(local)
+        for copy in copies:
+            copy.wait()
+        kernel(*views, *rest)
+
+    extra = [pltpu.VMEM(a.shape, a.dtype) for a in shapes]
+    return run, extra + [pltpu.SemaphoreType.DMA((len(shapes),))]
+
+
 def mid_kernel(q_count, z_count, x_ref, xe_ref, s_ref, se_ref, k_ref, d_ref, f_ref, spot_ref,
                gate_ref, tx_ref, ts_ref, rate_ref, skip_ref, gain_ref, out,
                pad_x, pad_s, values, writes, reads, mine_r, all_r, y, far, pd, far_pd, mixed, carried,
@@ -199,7 +223,7 @@
         pl.semaphore_signal(barrier, inc=1, device_id=peer(d), device_id_type=MESH)
     tokens, width = values.shape
     piece = tokens // q_count
-    heads = d_ref.shape[0]
+    heads = d_ref.shape[1]
     rows = mine_r.shape[0]
     taps = tx_ref.shape[0]
     has_edge = (z > 0).astype(f32)
@@ -243,7 +267,7 @@
         pad_x[EDGE + k * piece : EDGE + (k + 1) * piece, :] = x_ref[k].astype(f32)
     for k in range(q_count):
         filtered(pad_x, kernel_x, k * piece, values)
-    steps = d_ref[...]
+    steps = jnp.concatenate([d_ref[k] for k in range(q_count)], axis=1)
     lower = jnp.where(
         lax.broadcasted_iota(jnp.int32, (tokens, tokens), 0)
         <= lax.broadcasted_iota(jnp.int32, (tokens, tokens), 1),
@@ -344,13 +368,19 @@
 def middle(xs, x_edge, ss, s_edge, keeps, steps, flags, spots, gate, taps_x, taps_s, rate, skip, gain,
            q_count, z_count):
     f32, bf16 = jnp.float32, jnp.bfloat16
-    tokens = steps.shape[1]
+    tokens = steps.shape[0] * steps.shape[2]
     rows, width = gate.shape
+    operands = (
+        xs, x_edge, ss, s_edge, keeps, steps, flags, spots, gate, taps_x, taps_s, rate, skip, gain
+    )
+    run, extra = staged(
+        functools.partial(mid_kernel, q_count, z_count), (), len(operands), operands
+    )
     dma, vmem = pltpu.SemaphoreType.DMA, pltpu.VMEM
     return pl.pallas_call(
-        functools.partial(mid_kernel, q_count, z_count),
+        run,
         out_shape=jax.ShapeDtypeStruct((rows, width), bf16),
-        in_specs=[VMEM] * 14,
+        in_specs=[ANY] * len(operands),
         out_specs=VMEM,
         scratch_shapes=[
             vmem((EDGE + tokens, width), f32),
@@ -366,11 +396,11 @@
             vmem((z_count, 8, width), f32),
             vmem((rows, width), f32),
             vmem((rows, width), f32),
-        ] + [dma((z_count,))] * 6,
+        ] + [dma((z_count,))] * 6 + extra,
         compiler_params=pltpu.CompilerParams(
-            collective_id=1, has_side_effects=True, vmem_limit_bytes=50 * 1024 * 1024
+            collective_id=1, has_side_effects=True, vmem_limit_bytes=58 * 1024 * 1024
         ),
-    )(xs, x_edge, ss, s_edge, keeps, steps, flags, spots, gate, taps_x, taps_s, rate, skip, gain)
+    )(*operands)
 
 
 def tail_kernel(n, tp, q_count, z_count, n_ref, ow_ref, hw_ref, r_ref, g_ref, t_ref, p_ref, out,
@@ -560,10 +590,17 @@
         dma((z_count,)), dma((z_count,)), dma((e_n, z_count)), dma((e_n, z_count)),
         dma((x_n, z_count)), dma((x_n, z_count)),
     ]
+    operands = (
+        normed, out_weight, head_weight, res, gain[None], targets[:, None], policy[None]
+    )
+    run, extra = staged(
+        functools.partial(tail_kernel, n, tp, q_count, z_count), (1, 2), len(operands),
+        operands[:1] + operands[3:],
+    )
     result = pl.pallas_call(
-        functools.partial(tail_kernel, n, tp, q_count, z_count),
+        run,
         out_shape=jax.ShapeDtypeStruct((2, all_rows), f32),
-        in_specs=[VMEM, ANY, ANY, VMEM, VMEM, VMEM, VMEM],
+        in_specs=[ANY] * len(operands),
         out_specs=VMEM,
         scratch_shapes=[
             vmem(out_weight.shape, bf16),
@@ -576,11 +613,11 @@
             vmem((8, all_rows), f32),
             vmem((total, 8, all_rows), f32),
             dma((2,)), dma((tp,)), dma((tp,)), dma((total,)), dma((total,)),
-        ] + sems + sems,
+        ] + sems + sems + extra,
         compiler_params=pltpu.CompilerParams(
-            collective_id=3, has_side_effects=True, vmem_limit_bytes=50 * 1024 * 1024
+            collective_id=3, has_side_effects=True, vmem_limit_bytes=58 * 1024 * 1024
         ),
-    )(normed, out_weight, head_weight, res, gain[None], targets[:, None], policy[None])
+    )(*operands)
     return result[0], result[1]
 
 
@@ -627,7 +664,6 @@
     width = xs.shape[2]
     heads = ds.shape[1]
     rows = q_count * picked_rows
-    steps = ds.transpose(1, 0, 2).reshape(heads, tokens)
     gate = gs.reshape(rows, width)
     flags = ms[:, 0].reshape(tokens)
     spots = ms[:, 1, :picked_rows] + (jnp.arange(q_count) * rows_here).astype(f32)[:, None]
@@ -640,7 +676,7 @@
         keeping.append(keeping[-1] * clear[margin - offset + 1 : margin - offset + 1 + tokens])
     keeps = jnp.pad(jnp.stack(keeping), ((0, -taps % 8), (0, 0)))
     normed = middle(
-        xs, x_edge, ss, s_edge, keeps, steps, jnp.broadcast_to(flags[None], (8, tokens)), spots, gate,
+        xs, x_edge, ss, s_edge, keeps, ds, jnp.broadcast_to(flags[None], (8, tokens)), spots, gate,
         conv_inner, conv_state, decay_rate.reshape(q_count, heads, 1),
         skip_gain.reshape(q_count, 1, heads), norm_gain[None], q_count, z_count,
     )

time: 126 us -> 122 us (0.968)
  local copies, waits for them, and re-layouts: 17.1 us -> 9.49 us
  Pallas kernels: 102 us -> 106 us
    unnamed x28 -> x4, local copies, waits for them, and re-layouts: 11.6 us -> 1.06 us
    pallas_call x2, Pallas kernels: 74.4 us -> 78 us  [the longest x1 57.6 us: tail(): pl.pallas_call(run, out_shape=jax.ShapeDtypeStruct((2, all_rows), f32), i...]
where the time goes in v3:
time: 122 us
  Pallas kernels  106 us (87%)
  local copies, waits for them, and re-layouts  9.49 us (8%)
  other arithmetic  3.01 us (2%)
  matrix products  2.8 us (2%)
    pallas_call x1, Pallas kernels, tail(): pl.pallas_call(run, out_shape=jax.ShapeDtypeStruct((2, all_rows), f32), i...  57.6 us
    pallas_call x1, Pallas kernels, spread(): pl.pallas_call(functools.partial(spread_kernel, n, tp, q_count, z_count),...  27.9 us
    pallas_call x1, Pallas kernels, middle(): pl.pallas_call(run, out_shape=jax.ShapeDtypeStruct((rows, width), bf16),...  20.4 us

profile of v3, /device:TPU:0, one launch (start us, length us, event | category | flops | bytes accessed | tf_op | source)
XLA Modules:
  0.0 122.0 jit_solution(12821533674362735497)
XLA Ops:
  0.6 0.0 copy-start
  0.7 0.7 convert_bitcast_fusion
  1.4 0.5 copy-done
  1.9 0.9 convolution_convert_fusion.g_ref
  2.8 1.9 %convolution_convert_fusion.1 = bf16[8,2048]{1,0:T(8,128)(2,1)} fusion(bf16[128,2048]{1,0:T(8,128)(2,1)} %param.32, s32[8]{0:T(128)S(1)} %get-tuple-element.47), kind=kOutput, calls=%fused_computation.1 | convolution fusion | flops 4211712 | bytes 557088 | tf_op jit(solution)/shard_map/dot_general | solution.py:656
  4.7 0.7 convert_bitcast_fusion.1
  5.3 0.1 scatter.9.m_ref
  5.4 0.0 copy-start.1
  5.4 0.6 copy-done.1
  6.0 27.9 %shard_map.176 = (bf16[4,128,1024]{2,1,0:T(8,128)(2,1)}, bf16[4,2,128,128]{3,2,1,0:T(8,128)(2,1)}, f32[4,16,128]{2,1,0:T(8,128)}, bf16[4,8,1024]{2,1,0:T(8,128)(...) custom-call(bf16[128,4096]{1,0:T(8,128)(2,1)} %x_ref.1, ...), custom_call_target="tpu_custom_call" | custom-call | tf_op jit(solution)/shard_map/pallas_call | solution.py:173
  34.0 0.8 fusion.2
  34.7 0.7 slice.58
  35.4 0.1 maximum_subtract_fusion
  35.5 0.1 slice_multiply_fusion
  35.6 0.1 pad_maximum_fusion
  35.7 0.6 pad.10.refs_4_
  36.3 0.6 broadcast_in_dim.26.refs_6_
  36.9 0.7 slice_reduce_fusion
  37.6 0.1 squeeze.10
  37.7 0.1 add.27
  37.8 0.1 add.28
  37.9 0.1 copy.24
  38.0 0.6 convert_element_type.30.refs_7_
  38.6 1.4 %reshape.118.refs_11_ = f32[4,16,1]{2,1,0:T(8,128)} reshape(f32[64]{0:T(128)} %param.26) | data formatting | bytes 512 | tf_op jit(solution)/shard_map/reshape | solution.py:680
  40.0 1.3 %reshape.116 = f32[4,1,16]{2,0,1:T(4,128)} reshape(f32[64]{0:T(128)} %param.27) | data formatting | bytes 512 | tf_op jit(solution)/shard_map/reshape | solution.py:681
  41.3 20.4 %shard_map.177.refs_0_ = bf16[32,1024]{1,0:T(8,128)(2,1)} custom-call(bf16[4,128,1024]{2,1,0:T(8,128)(2,1)} %get-tuple-element.35.refs_0_, bf16[16,1024]{1,0:T(8,128)(2,1)} %get-tuple-element.36.refs_1_, bf16[4,2,128,128]{3,2,1,0:T(8,128)(2,1)} %get-tuple-element.37.refs_2_, bf16[2,16,128]{2,1,0:T(8,128)(2,1)} %get-tuple-element.38.refs_3_, ...), custom_call_target="tpu_custom_call" | custom-call | tf_op jit(solution)/shard_map/pallas_call | solution.py:380
  61.8 1.4 %copy.27.refs_5_ = s32[128,1]{1,0:T(8,128)} copy(s32[128,1]{0,1:T(1,128)} %bitcast.39) | data formatting | bytes 1024 | tf_op jit(solution)/shard_map/broadcast_in_dim | solution.py:594
  63.1 57.6 %shard_map.178 = f32[2,128]{1,0:T(2,128)} custom-call(bf16[32,1024]{1,0:T(8,128)(2,1)} %shard_map.177.refs_0_, bf16[4096,256]{1,0:T(8,128)(2,1)} %refs_1_.1, bf16[4096,2048]{1,0:T(8,128)(2,1)} %refs_2_.1, bf16[128,256]{1,0:T(8,128)(2,1)} %bitcast.28, f32[1,4096]{1,0:T(1,128)} %bitcast.33, s32[128,1]{1,0:T(8,128)} %copy.27.refs_5_, f32[1,128]{1,0:T(1,128)} %bitcast.38), custom_call_target="tpu_custom_call" | custom-call | tf_op jit(solution)/shard_map/pallas_call | solution.py:600
  120.7 1.2 %slice_bitcast_fusion = (f32[128]{0:T(128)}, f32[128]{0:T(128)}) fusion(f32[2,128]{1,0:T(2,128)} %shard_map.178), kind=kLoop, calls=%fused_computation.12 | loop fusion | bytes 2048 | tf_op jit(solution)/shard_map/squeeze | solution.py:621
  (4 shorter events, 0.0 us)
Async XLA Ops:
  0.6 1.2 %copy-start = (bf16[128,4096]{1,0:T(8,128)(2,1)S(1)}, bf16[128,4096]{1,0:T(8,128)(2,1)}, u32[]{:S(2)}) copy-start(bf16[128,4096]{1,0:T(8,128)(2,1)} %param.22) | copy-start | bytes 3145732
  5.4 0.6 copy-start.1
